TPU v7x, 32 devices: a whole 2x2x4 slice. The times are simulated.
32 devices in a mesh: tm: 16 (over z, y, x), row: 2 (over core).
Axes of the slice: x: 2, y: 2, z: 4, core: 2. Of those that a mesh axis runs over, the one named last changes fastest.
Arguments:
- transition: bfloat16 [16, 896, 896], P('tm', 'row'), as said below
- offsets: float32 [16, 896, 128], P('tm', 'row'), may hold values from -0.72 to 0.72
- start: float32 [896, 128], P('row'), may hold values from -6 to 6
Outputs:
- states: float32 [16, 896, 128], P('tm', 'row')
Inputs may be any that keep to these rules, and one draw needn't show every extreme that they name: The products of consecutive transition matrices stay bounded.
All inputs are finite; a program needn't handle non-finite values.
Results may differ from a plain program's by a relative error of at most 0.0003.
Values sent between devices are 32-bit elements; how exact they have to be, the bound alone decides.
No kernel may reach another device: no remote copies, remote signals or barrier semaphores. Data moves between devices by JAX's collectives and lax.ppermute only.
A program may use at most 64 MiB of HBM per device.

v0:
```python
import jax
import jax.numpy as jnp
from jax import lax
from jax.sharding import PartitionSpec as P


def from_behind(block, axis, distance):
    devices = range(lax.axis_size(axis))
    route = [((i - distance) % len(devices), i) for i in devices]
    return lax.ppermute(block, axis, route)


def exact_product(matrix, columns):
    return jnp.dot(
        matrix, columns, precision=lax.Precision.HIGHEST, preferred_element_type=jnp.float32
    )


def local(transition, offsets, start):
    carry_matrix = transition[0].astype(jnp.float32)
    carry_offset = offsets[0]
    panel_rows_count = carry_matrix.shape[0]
    full_order = carry_matrix.shape[1]
    position = lax.axis_index("tm")
    row_first = lax.axis_index("row") * panel_rows_count
    row_ids = lax.broadcasted_iota(jnp.int32, (panel_rows_count, full_order), 0) + row_first
    col_ids = lax.broadcasted_iota(jnp.int32, (panel_rows_count, full_order), 1)
    identity_panel = (row_ids == col_ids).astype(jnp.float32)
    levels = lax.axis_size("tm").bit_length() - 1
    for level_index in range(levels):
        distance = 1 << level_index
        present = position >= distance
        moved_offset = from_behind(carry_offset, "tm", distance)
        moved_matrix = from_behind(carry_matrix, "tm", distance)
        moved_offset = jnp.where(present, moved_offset, jnp.zeros_like(moved_offset))
        moved_matrix = jnp.where(present, moved_matrix, identity_panel)
        whole_offset = lax.all_gather(moved_offset, "row", axis=0, tiled=True)
        whole_matrix = lax.all_gather(moved_matrix, "row", axis=0, tiled=True)
        next_offset = exact_product(carry_matrix, whole_offset) + carry_offset
        carry_matrix = exact_product(carry_matrix, whole_matrix)
        carry_offset = next_offset
    whole_start = lax.all_gather(start, "row", axis=0, tiled=True)
    result = exact_product(carry_matrix, whole_start) + carry_offset
    return result[None]


def solution(mesh):
    in_specs = (P("tm", "row", None), P("tm", "row", None), P("row", None))
    out_specs = P("tm", "row", None)
    return jax.shard_map(local, mesh=mesh, in_specs=in_specs, out_specs=out_specs, check_vma=False)
```

profile of v0, /device:TPU:0, one launch (start us, length us, event | category | flops | bytes accessed | tf_op | source)
XLA Modules:
  0.0 340.5 jit_solution(16006621053571129460)
XLA Ops:
  6.5 1.2 bitcast_convert_fusion
  7.8 3.0 collective-permute-start
  10.8 39.1 %collective-permute-done = f32[448,896]{1,0:T(8,128)S(1)} collective-permute-done((f32[448,896]{1,0:T(8,128)S(1)}, f32[448,896]{1,0:T(8,128)S(1)}, u32[]{:S(2)}, u32[]{:S(2)}) %collective-permute-start) | collective-permute-done | bytes 1605664 | tf_op jit(solution)/shard_map/ppermute | solution.py:10
  49.9 1.4 convert_select_fusion.3
  51.3 0.0 all-gather.5.cloned.1.call-update
  51.3 0.0 all-gather.7.cloned.1.call-start
  51.4 9.8 %all-gather.5.cloned.1.call-done = f32[896,896]{1,0:T(8,128)} async-done(((f32[448,896]{1,0:T(8,128)}), f32[896,896]{1,0:T(8,128)}) %all-gather.5.cloned.1.call-update) | async-done | bytes 3211280 | tf_op jit(solution)/shard_map/all_gather | solution.py:38
  61.2 4.9 %fusion.4 = f32[896,448]{0,1:T(8,128)S(1)} fusion(f32[896,896]{1,0:T(8,128)} %all-gather.5.cloned.1.call-done, bf16[1,448,896]{2,1,0:T(8,128)(2,1)S(1)} %copy-done), kind=kOutput, calls=%fused_computation.13 | convolution fusion | flops 4315938816 | bytes 5619712 | tf_op jit(solution)/shard_map/dot_general | solution.py:14
  66.1 1.8 collective-permute-start.1
  67.9 38.3 %collective-permute-done.1 = f32[448,896]{1,0:T(8,128)S(1)} collective-permute-done((f32[448,896]{1,0:T(8,128)S(1)}, f32[448,896]{1,0:T(8,128)S(1)}, u32[]{:S(2)}, u32[]{:S(2)}) %collective-permute-start.1) | collective-permute-done | bytes 1605664 | tf_op jit(solution)/shard_map/ppermute | solution.py:10
  106.3 1.4 convert_select_fusion.2
  107.7 0.0 all-gather.7.cloned.1.call-update
  107.7 0.0 all-gather.9.cloned.1.call-start
  107.7 10.7 %all-gather.7.cloned.1.call-done = f32[896,896]{1,0:T(8,128)} async-done(((f32[448,896]{1,0:T(8,128)}), f32[896,896]{1,0:T(8,128)}) %all-gather.7.cloned.1.call-update) | async-done | bytes 3211280 | tf_op jit(solution)/shard_map/all_gather | solution.py:38
  118.5 7.8 %fusion.6 = f32[448,896]{1,0:T(8,128)S(1)} fusion(f32[896,448]{0,1:T(8,128)S(1)} %fusion.4, f32[896,896]{1,0:T(8,128)} %all-gather.7.cloned.1.call-done), kind=kOutput, calls=%fused_computation.21 | convolution fusion | flops 4315938816 | bytes 6422528 | tf_op jit(solution)/shard_map/dot_general | solution.py:14
  126.3 1.8 collective-permute-start.2
  128.1 37.5 %collective-permute-done.2 = f32[448,896]{1,0:T(8,128)} collective-permute-done((f32[448,896]{1,0:T(8,128)S(1)}, f32[448,896]{1,0:T(8,128)}, u32[]{:S(2)}, u32[]{:S(2)}) %collective-permute-start.2) | collective-permute-done | bytes 1605664 | tf_op jit(solution)/shard_map/ppermute | solution.py:10
  165.6 1.4 convert_select_fusion.1
  167.0 0.0 all-gather.9.cloned.1.call-update
  167.0 0.2 all-gather.11.cloned.1.call-start
  167.2 12.9 %all-gather.9.cloned.1.call-done = f32[896,896]{1,0:T(8,128)} async-done(((f32[448,896]{1,0:T(8,128)}), f32[896,896]{1,0:T(8,128)}) %all-gather.9.cloned.1.call-update) | async-done | bytes 3211280 | tf_op jit(solution)/shard_map/all_gather | solution.py:38
  180.1 8.6 %fusion.7 = f32[448,896]{1,0:T(8,128)} fusion(f32[448,896]{1,0:T(8,128)S(1)} %fusion.6, f32[896,896]{1,0:T(8,128)} %all-gather.9.cloned.1.call-done), kind=kOutput, calls=%fused_computation.22 | convolution fusion | flops 4315938816 | bytes 6422528 | tf_op jit(solution)/shard_map/dot_general | solution.py:14
  188.7 2.7 collective-permute-start.3
  191.3 70.3 %collective-permute-done.3 = f32[448,896]{1,0:T(8,128)} collective-permute-done((f32[448,896]{1,0:T(8,128)}, f32[448,896]{1,0:T(8,128)}, u32[]{:S(2)}, u32[]{:S(2)}) %collective-permute-start.3) | collective-permute-done | bytes 1605664 | tf_op jit(solution)/shard_map/ppermute | solution.py:10
  261.6 1.5 convert_select_fusion
  263.1 0.0 all-gather.11.cloned.1.call-update
  263.1 0.0 copy-start.1
  263.1 0.9 copy-done.2
  264.0 1.7 collective-permute-start.4
  265.7 10.9 %collective-permute-done.4 = f32[448,128]{1,0:T(8,128)S(1)} collective-permute-done((f32[448,128]{1,0:T(8,128)S(1)}, f32[448,128]{1,0:T(8,128)S(1)}, u32[]{:S(2)}, u32[]{:S(2)}) %collective-permute-start.4) | collective-permute-done | bytes 229408 | tf_op jit(solution)/shard_map/ppermute | solution.py:10
  276.6 2.1 all_gather.32
  278.8 0.8 fusion
  279.5 0.1 collective-permute-start.5
  279.6 10.3 %collective-permute-done.5 = f32[448,128]{1,0:T(8,128)S(1)} collective-permute-done((f32[448,128]{1,0:T(8,128)S(1)}, f32[448,128]{1,0:T(8,128)S(1)}, u32[]{:S(2)}, u32[]{:S(2)}) %collective-permute-start.5) | collective-permute-done | bytes 229408 | tf_op jit(solution)/shard_map/ppermute | solution.py:10
  290.0 2.1 all_gather.33
  292.1 1.5 convolution_add_fusion.2
  293.6 0.1 collective-permute-start.6
  293.6 9.4 %collective-permute-done.6 = f32[448,128]{1,0:T(8,128)S(1)} collective-permute-done((f32[448,128]{1,0:T(8,128)S(1)}, f32[448,128]{1,0:T(8,128)S(1)}, u32[]{:S(2)}, u32[]{:S(2)}) %collective-permute-start.6) | collective-permute-done | bytes 229408 | tf_op jit(solution)/shard_map/ppermute | solution.py:10
  303.1 0.0 copy-start.3
  303.1 2.3 all_gather.34
  305.4 1.5 convolution_add_fusion.1
  306.8 0.1 collective-permute-start.7
  306.9 2.1 all_gather.31
  309.0 9.2 %collective-permute-done.7 = f32[448,128]{1,0:T(8,128)S(1)} collective-permute-done((f32[448,128]{1,0:T(8,128)S(1)}, f32[448,128]{1,0:T(8,128)S(1)}, u32[]{:S(2)}, u32[]{:S(2)}) %collective-permute-start.7) | collective-permute-done | bytes 229408 | tf_op jit(solution)/shard_map/ppermute | solution.py:10
  318.3 2.4 all_gather.35
  320.6 8.3 %fusion.8 = f32[448,896]{1,0:T(8,128)S(1)} fusion(f32[448,896]{1,0:T(8,128)} %fusion.7, f32[896,896]{1,0:T(8,128)} %all-gather.11.cloned.1.call-done), kind=kOutput, calls=%fused_computation.23 | convolution fusion | flops 4315938816 | bytes 6422528 | tf_op jit(solution)/shard_map/dot_general | solution.py:14
  328.9 1.5 fusion.9
  330.4 3.6 %fusion.2 = f32[1,448,128]{2,1,0:T(8,128)} fusion(f32[448,128]{1,0:T(8,128)S(1)} %fusion.9, f32[448,128]{1,0:T(8,128)S(1)} %convolution_add_fusion.1, f32[448,896]{1,0:T(8,128)} %fusion.7, f32[896,128]{1,0:T(8,128)S(1)} %all_gather.35), kind=kOutput, calls=%fused_computation.9 | convolution fusion | flops 616677376 | bytes 2752512 | tf_op jit(solution)/shard_map/dot_general | solution.py:14
  (12 shorter events, 0.1 us)
Async XLA Ops:
  6.5 54.7 %all-gather.5.cloned.1.call-start = ((), (), s32[]{:S(2)}) async-start(), calls=%async_computation | async-start | bytes 4816896 | tf_op jit(solution)/shard_map/all_gather | solution.py:38
  7.8 42.1 %collective-permute-start = (f32[448,896]{1,0:T(8,128)S(1)}, f32[448,896]{1,0:T(8,128)S(1)}, u32[]{:S(2)}, u32[]{:S(2)}) collective-permute-start(f32[448,896]{1,0:T(8,128)S(1)} %bitcast_convert_fusion), channel_id=1, source_target_pairs={{30,0},{0,2},{2,4},{4,6},{6,8},{8,10},{10,12},{12,14},{14,16},{16,... | collective-permute-start | bytes 4816904 | tf_op jit(solution)/shard_map/ppermute | solution.py:10
  51.3 9.9 %copy-start = (bf16[1,448,896]{2,1,0:T(8,128)(2,1)S(1)}, bf16[1,448,896]{2,1,0:T(8,128)(2,1)}, u32[]{:S(2)}) copy-start(bf16[1,448,896]{2,1,0:T(8,128)(2,1)} %param.3) | copy-start | bytes 2408452
  51.3 67.1 %all-gather.7.cloned.1.call-start = ((), (), s32[]{:S(2)}) async-start(), calls=%async_computation.1 | async-start | bytes 4816896 | tf_op jit(solution)/shard_map/all_gather | solution.py:38
  66.1 40.1 %collective-permute-start.1 = (f32[448,896]{1,0:T(8,128)S(1)}, f32[448,896]{1,0:T(8,128)S(1)}, u32[]{:S(2)}, u32[]{:S(2)}) collective-permute-start(f32[448,896]{1,0:T(8,128)S(1)} %bitcast.31), channel_id=1, source_target_pairs={{28,0},{30,2},{0,4},{2,6},{4,8},{6,10},{8,12},{10,14},{12,16},{14,... | collective-permute-start | bytes 4816904 | tf_op jit(solution)/shard_map/ppermute | solution.py:10
  107.7 72.4 %all-gather.9.cloned.1.call-start = ((), (), s32[]{:S(2)}) async-start(), calls=%async_computation.2 | async-start | bytes 4816896 | tf_op jit(solution)/shard_map/all_gather | solution.py:38
  126.3 39.3 %collective-permute-start.2 = (f32[448,896]{1,0:T(8,128)S(1)}, f32[448,896]{1,0:T(8,128)}, u32[]{:S(2)}, u32[]{:S(2)}) collective-permute-start(f32[448,896]{1,0:T(8,128)S(1)} %fusion.6), channel_id=1, source_target_pairs={{24,0},{26,2},{28,4},{30,6},{0,8},{2,10},{4,12},{6,14},{8,16},{10,... | collective-permute-start | bytes 4816904 | tf_op jit(solution)/shard_map/ppermute | solution.py:10
  167.0 153.6 %all-gather.11.cloned.1.call-start = ((), (), s32[]{:S(2)}) async-start(), calls=%async_computation.3 | async-start | bytes 4816896 | tf_op jit(solution)/shard_map/all_gather | solution.py:38
  188.7 72.9 %collective-permute-start.3 = (f32[448,896]{1,0:T(8,128)}, f32[448,896]{1,0:T(8,128)}, u32[]{:S(2)}, u32[]{:S(2)}) collective-permute-start(f32[448,896]{1,0:T(8,128)} %fusion.7), channel_id=1, source_target_pairs={{16,0},{18,2},{20,4},{22,6},{24,8},{26,10},{28,12},{30,14},{0,16},... | collective-permute-start | bytes 4816904 | tf_op jit(solution)/shard_map/ppermute | solution.py:10
  263.1 0.9 copy-start.2
  263.1 15.7 %copy-start.1 = (bf16[1,448,896]{2,1,0:T(8,128)(2,1)S(1)}, bf16[1,448,896]{2,1,0:T(8,128)(2,1)}, u32[]{:S(2)}) copy-start(bf16[1,448,896]{2,1,0:T(8,128)(2,1)} %param.3) | copy-start | bytes 2408452
  264.0 12.6 %collective-permute-start.4 = (f32[448,128]{1,0:T(8,128)S(1)}, f32[448,128]{1,0:T(8,128)S(1)}, u32[]{:S(2)}, u32[]{:S(2)}) collective-permute-start(f32[448,128]{1,0:T(8,128)S(1)} %bitcast.32), channel_id=1, source_target_pairs={{30,0},{0,2},{2,4},{4,6},{6,8},{8,10},{10,12},{12,14},{14,16},{16,... | collective-permute-start | bytes 688136 | tf_op jit(solution)/shard_map/ppermute | solution.py:10
  279.5 10.4 %collective-permute-start.5 = (f32[448,128]{1,0:T(8,128)S(1)}, f32[448,128]{1,0:T(8,128)S(1)}, u32[]{:S(2)}, u32[]{:S(2)}) collective-permute-start(f32[448,128]{1,0:T(8,128)S(1)} %fusion), channel_id=1, source_target_pairs={{28,0},{30,2},{0,4},{2,6},{4,8},{6,10},{8,12},{10,14},{12,16},{14,... | collective-permute-start | bytes 688136 | tf_op jit(solution)/shard_map/ppermute | solution.py:10
  293.6 9.5 %collective-permute-start.6 = (f32[448,128]{1,0:T(8,128)S(1)}, f32[448,128]{1,0:T(8,128)S(1)}, u32[]{:S(2)}, u32[]{:S(2)}) collective-permute-start(f32[448,128]{1,0:T(8,128)S(1)} %convolution_add_fusion.2), channel_id=1, source_target_pairs={{24,0},{26,2},{28,4},{30,6},{0,8},{2,10},{4,12},{6,14},{8,16},{10,... | collective-permute-start | bytes 688136 | tf_op jit(solution)/shard_map/ppermute | solution.py:10
  303.1 3.8 %copy-start.3 = (f32[448,128]{1,0:T(8,128)S(1)}, f32[448,128]{1,0:T(8,128)}, u32[]{:S(2)}) copy-start(f32[448,128]{1,0:T(8,128)} %param.5) | copy-start | bytes 688132
  306.8 11.4 %collective-permute-start.7 = (f32[448,128]{1,0:T(8,128)S(1)}, f32[448,128]{1,0:T(8,128)S(1)}, u32[]{:S(2)}, u32[]{:S(2)}) collective-permute-start(f32[448,128]{1,0:T(8,128)S(1)} %convolution_add_fusion.1), channel_id=1, source_target_pairs={{16,0},{18,2},{20,4},{22,6},{24,8},{26,10},{28,12},{30,14},{0,16},... | collective-permute-start | bytes 688136 | tf_op jit(solution)/shard_map/ppermute | solution.py:10
Sparse Core Ops, SparseCore 0:
  51.5 9.7 all-gather.4
  107.8 10.6 all-gather.6
  167.1 12.9 all-gather.8
  263.2 14.7 all-gather.10
where the time goes:
time: 341 us; the launch traced here: 340 us
  waiting for transfers between devices  259 us (76%)
  matrix products  38.2 us (11%)
  between operations  13.2 us (4%)
  starting transfers between devices  11.5 us (3%)
  blocking collectives  11 us (3%)
  other arithmetic  7.03 us (2%)
    ppermute x8, waiting for transfers between devices, from_behind(): return lax.ppermute(block, axis, route)  225 us
    dot_general x9, matrix products, exact_product(): jnp.dot(matrix, columns, precision=lax.Precision.HIGHEST, preferred_eleme...  38.2 us
    all_gather x4, waiting for transfers between devices, local(): whole_matrix = lax.all_gather(moved_matrix, 'row', axis=0, tiled=True)  33.4 us
    ppermute x8, starting transfers between devices, from_behind(): return lax.ppermute(block, axis, route)  11.2 us
    all_gather x4, blocking collectives, local(): whole_offset = lax.all_gather(moved_offset, 'row', axis=0, tiled=True)  8.89 us
  transfers between devices with their start and end apart: 12, of which 11 were waited for; matrix products, arithmetic and copies ran while one was open for 1% of the time, Pallas kernels for 0%

commit v1 on v0

v1 whole, which is shorter than its diff:
```python
import functools

import jax
import jax.numpy as jnp
from jax import lax
from jax.experimental import pallas as pl
from jax.experimental.pallas import tpu as pltpu
from jax.sharding import PartitionSpec as P


CHUNKS = 2
SINGLE = 8
ANY = pl.BlockSpec(memory_space=pl.ANY)
HBM = pl.BlockSpec(memory_space=pltpu.HBM)
VMEM = pl.BlockSpec(memory_space=pltpu.VMEM)
F32, BF16 = jnp.float32, jnp.bfloat16


def route_of(to, spare):
    slices, rows = lax.axis_size("tm"), lax.axis_size("row")
    route = []
    for i in range(slices):
        for r in range(rows):
            if i in to:
                route.append((i * rows + r, to[i] * rows + r))
            elif spare:
                route.append((i * rows + r, i * rows + (r + 1) % rows))
    return route


def hop(block, pairs):
    to = {}
    for a, b in pairs:
        to[a], to[b] = b, a
    return lax.ppermute(block, ("tm", "row"), route_of(to, True))


def ship(block, evens):
    return lax.ppermute(block, ("tm", "row"), route_of({e: e + 1 for e in evens}, False))


def swap_cores(block, places=None):
    rows = lax.axis_size("row")
    places = range(lax.axis_size("tm")) if places is None else places
    route = [(i * rows + r, i * rows + (r + 1) % rows) for i in places for r in range(rows)]
    return lax.ppermute(block, ("tm", "row"), route)


def call(kernel, operands, specs, outs, aliases=None, flops=0, limit=8, scratch=()):
    moved = sum(o.size * o.dtype.itemsize for o in outs)
    return pl.pallas_call(
        kernel,
        out_shape=tuple(outs),
        in_specs=specs,
        out_specs=tuple([VMEM] * len(outs)),
        scratch_shapes=scratch,
        input_output_aliases=aliases or {},
        compiler_params=pltpu.CompilerParams(vmem_limit_bytes=limit << 20),
        cost_estimate=pl.CostEstimate(flops=flops, bytes_accessed=moved, transcendentals=0),
    )(*operands)


def gate(block, *after):
    def kernel(*refs):
        del refs

    return pl.pallas_call(
        kernel,
        out_shape=jax.ShapeDtypeStruct(block.shape, block.dtype),
        in_specs=[ANY] * (1 + len(after)),
        out_specs=ANY,
        input_output_aliases={0: 0},
        compiler_params=pltpu.CompilerParams(vmem_limit_bytes=1 << 20),
        name="gate",
    )(block, *after)


def is_any(places):
    here = lax.axis_index("tm")
    found = here == places[0]
    for place in places[1:]:
        found = jnp.logical_or(found, here == place)
    return found


def first_core():
    return lax.axis_index("row") == 0


def both_halves(mine, other):
    first = first_core()
    return jnp.concatenate(
        [jnp.where(first, mine, other), jnp.where(first, other, mine)], axis=0
    )


def own_columns(mine, other):
    across = both_halves(mine, other).T
    half = mine.shape[1] // 2
    return jnp.where(first_core(), across[:half], across[half:])


def split_product(x, matrix):
    rows = x.shape[0]
    high = x.astype(BF16)
    low = (x - high.astype(F32)).astype(BF16)
    product = jnp.dot(
        jnp.concatenate([high, low], axis=0), matrix, preferred_element_type=F32
    )
    return product[:rows] + product[rows:]


def first_kernel(own_ref, offset_ref, start_ref, other_start_ref, keep_ref, give_ref):
    @pl.when(is_any([0]))
    def _():
        x = both_halves(start_ref[...], other_start_ref[...]).T
        high = x.astype(BF16)
        low = (x - high.astype(F32)).astype(BF16)
        across = (((1,), (1,)), ((), ()))
        y = lax.dot_general(high, own_ref[...], across, preferred_element_type=F32)
        y += lax.dot_general(low, own_ref[...], across, preferred_element_type=F32)
        y += offset_ref[...].T
        half = y.shape[0] // 2
        first = first_core()
        keep_ref[...] = jnp.where(first, y[:half], y[half:])
        give_ref[...] = jnp.where(first, y[half:], y[:half])


def join_kernel(keep_ref, got_ref, *y_refs):
    @pl.when(is_any([0]))
    def _():
        first = first_core()
        keep, got = keep_ref[...], got_ref[...]
        y = jnp.concatenate(
            [jnp.where(first, keep, got), jnp.where(first, got, keep)], axis=1
        )
        chunk = y_refs[0].shape[0]
        for c in range(CHUNKS):
            y_refs[c][...] = y[c * chunk : (c + 1) * chunk]


def begin_kernel(own_ref, offset_ref, other_ref, other_offset_ref, matrix_ref, columns_ref):
    own = own_ref[...].astype(F32)
    matrix_ref[...] = both_halves(own, other_ref[...]).T.astype(BF16)
    columns_ref[...] = own_columns(offset_ref[...], other_offset_ref[...])


def migrate_kernel(odds, own_ref, other_ref, matrix_ref):
    @pl.when(is_any(odds))
    def _():
        matrix_ref[...] = both_halves(own_ref[...], other_ref[...]).T.astype(BF16)


def step_kernel(c, plan, alias, x_refs, matrix_ref, offset_ref, got_ref, got_offset_ref, before_ref, y_ref):
    chunk = y_ref.shape[0]
    here = pl.ds(c * chunk, chunk)
    everyone = [place for places in plan.values() for place in places]
    for (source, double), places in plan.items():

        @pl.when(is_any(places))
        def _(source=source, double=double):
            x = x_refs[source][...]
            if double:
                x = split_product(x, got_ref[...]) + got_offset_ref[here]
            y_ref[...] = split_product(x, matrix_ref[...]) + offset_ref[here]

    if not alias:

        @pl.when(jnp.logical_not(is_any(everyone)))
        def _():
            y_ref[...] = before_ref[...]


def local(transition, offsets, start):
    slices = lax.axis_size("tm")
    own, offset = transition[0], offsets[0]
    part, order = own.shape
    columns = start.shape[1]
    half = columns // 2
    chunk = half // CHUNKS
    shape = jax.ShapeDtypeStruct
    piece = shape((chunk, order), F32)
    evens = list(range(SINGLE, slices, 2))
    odds = [e + 1 for e in evens]
    product = 4 * chunk * order * order

    block = shape((half, part), F32)
    other_start = swap_cores(start)
    wide = own.astype(F32)
    shipped = ship(wide, evens)
    keep, give = call(
        first_kernel, (own, offset, start, other_start), [VMEM] * 4, [block] * 2,
        flops=4 * columns * part * order, limit=16,
    )
    got = swap_cores(give)
    ys = list(call(join_kernel, (keep, got), [VMEM] * 2, [piece] * CHUNKS))
    other = swap_cores(wide)
    other_offset = swap_cores(offset)
    matrix, offset = call(
        begin_kernel, (own, offset, other, other_offset), [VMEM] * 4,
        [shape((order, order), BF16), shape((half, order), F32)], limit=24,
    )
    got_offset = ship(offset, evens)

    def step(c, xs, plan, got=(), after=(), alias=True):
        double = len(got) > 0
        count = len(xs)

        def kernel(*refs):
            x_refs, refs = refs[:count], refs[count:]
            before_ref, matrix_ref, offset_ref = refs[:3]
            got_ref, got_offset_ref = refs[3:5] if double else (None, None)
            step_kernel(c, plan, alias, x_refs, matrix_ref, offset_ref, got_ref, got_offset_ref, before_ref, refs[-1])

        after = (ys[c - 1], *after)
        (ys[c],) = call(
            kernel,
            (*xs, ys[c], matrix, offset, *got, *after),
            [VMEM] * (count + 3 + len(got)) + [ANY] * len(after), [piece],
            aliases={count: 0} if alias else None, flops=product * (1 + double),
        )

    def move(c, pairs):
        return hop(ys[c], pairs)

    for stage in range(1, SINGLE):
        if stage == SINGLE - 1:
            shipped = gate(shipped, *ys)
            shipped_other = swap_cores(shipped)
            (moved,) = call(
                functools.partial(migrate_kernel, odds), (shipped, shipped_other), [VMEM] * 2,
                [shape((order, order), BF16)], limit=24,
            )
        for c in range(CHUNKS):
            x = move(c, [(stage - 1, stage)])
            step(c, [x], {(0, False): [stage]})
    for odd in odds:
        last = odd == slices - 1
        pairs = [(odd - 2, odd)] + ([(odd - 4, odd - 3)] if odd > odds[0] else [])
        plan = {(0, True): [odd]}
        if odd > odds[0]:
            plan[(0, False)] = [odd - 3]
        if last:
            plan[(1, False)] = [odd - 1]
        for c in range(CHUNKS):
            xs = [move(c, pairs)] + ([move(c, [(odd - 2, odd - 1)])] if last else [])
            step(c, xs, plan, got=(moved, got_offset), alias=not last)

    def give_kernel(*refs):
        y = jnp.concatenate([ref[...] for ref in refs[:CHUNKS]], axis=0)
        refs[-1][...] = jnp.where(first_core(), y[:, part:], y[:, :part])

    def end_kernel(*refs):
        y = jnp.concatenate([ref[...] for ref in refs[:CHUNKS]], axis=0)
        first = first_core()
        mine = jnp.where(first, y[:, :part], y[:, part:])
        taken = refs[CHUNKS][...]
        rows = jnp.concatenate(
            [jnp.where(first, mine, taken), jnp.where(first, taken, mine)], axis=0
        )
        refs[-1][...] = rows.T

    (give,) = call(give_kernel, tuple(ys), [VMEM] * CHUNKS, [shape((half, part), F32)])
    (out,) = call(
        end_kernel, (*ys, swap_cores(give)), [VMEM] * (CHUNKS + 1), [shape((part, columns), F32)]
    )
    return out[None]


def solution(mesh):
    in_specs = (P("tm", "row", None), P("tm", "row", None), P("row", None))
    out_specs = P("tm", "row", None)
    return jax.shard_map(local, mesh=mesh, in_specs=in_specs, out_specs=out_specs, check_vma=False)
```

time: 341 us -> 78.1 us (0.23)
  the two profiles are of different devices: /device:TPU:0 before, /device:TPU:27 now
where the time goes in v1:
time: 78.1 us; the launch traced here: 78 us
  waiting for transfers between devices  48.8 us (62%)
  starting transfers between devices  24 us (31%)
  Pallas kernels  3.72 us (5%)
  other arithmetic  1.34 us (2%)
    ppermute x2, waiting for transfers between devices, ship(): lax.ppermute(block, ('tm', 'row'), route_of({e: e + 1 for e in evens}, Fa...  29.6 us
    ppermute x24, starting transfers between devices, hop(): return lax.ppermute(block, ('tm', 'row'), route_of(to, True))  17.3 us
    ppermute x24, waiting for transfers between devices, hop(): return lax.ppermute(block, ('tm', 'row'), route_of(to, True))  15.3 us
    ppermute x6, starting transfers between devices, swap_cores(): return lax.ppermute(block, ('tm', 'row'), route)  4.09 us
    ppermute x6, waiting for transfers between devices, swap_cores(): return lax.ppermute(block, ('tm', 'row'), route)  3.87 us
    pallas_call x28, Pallas kernels, call(): pl.pallas_call(kernel, out_shape=tuple(outs), in_specs=specs, out_specs=t...  3.72 us
    ppermute x2, starting transfers between devices, ship(): lax.ppermute(block, ('tm', 'row'), route_of({e: e + 1 for e in evens}, Fa...  2.56 us
  transfers between devices with their start and end apart: 32, of which 16 were waited for; matrix products, arithmetic and copies ran while one was open for 0% of the time, Pallas kernels for 3%

profile of v1, /device:TPU:27, one launch (start us, length us, event | category | flops | bytes accessed | tf_op | source)
XLA Modules:
  0.0 78.0 jit_solution(5153848515150443160)
XLA Ops:
  0.0 1.3 %bitcast_convert_fusion = f32[448,896]{1,0:T(8,128)S(1)} fusion(bf16[1,448,896]{2,1,0:T(8,128)(2,1)} %param.3), kind=kLoop, calls=%fused_computation | loop fusion | flops 401408 | bytes 2408448 | tf_op jit(solution)/shard_map/convert_element_type | solution.py:189
  1.4 0.7 collective-permute-start.3
  2.1 1.3 %collective-permute-start.18 = (f32[448,896]{1,0:T(8,128)S(1)}, f32[448,896]{1,0:T(8,128)S(1)}, u32[]{:S(2)}, u32[]{:S(2)}) collective-permute-start(f32[448,896]{1,0:T(8,128)S(1)} %bitcast_convert_fusion), channel_id=1, source_target_pairs={{16,18},{17,19},{20,22},{21,23},{24,26},{25,27},{28,30},{29,31}} | collective-permute-start | bytes 4816904 | tf_op jit(solution)/shard_map/ppermute | solution.py:39
  3.5 2.0 %collective-permute-done.other_start_ref = f32[448,128]{1,0:T(8,128)S(1)} collective-permute-done((f32[448,128]{1,0:T(8,128)S(1)}, f32[448,128]{1,0:T(8,128)S(1)}, u32[]{:S(2)}, u32[]{:S(2)}) %collective-permute-start) | collective-permute-done | bytes 229408 | tf_op jit(solution)/shard_map/ppermute | solution.py:46
  5.5 0.4 collective-permute-start.1
  6.0 0.8 %collective-permute-done.1.got_ref = f32[64,448]{1,0:T(8,128)S(1)} collective-permute-done((f32[64,448]{1,0:T(8,128)S(1)}, f32[64,448]{1,0:T(8,128)S(1)}, u32[]{:S(2)}, u32[]{:S(2)}) %collective-permute-start.1) | collective-permute-done | bytes 114720 | tf_op jit(solution)/shard_map/ppermute | solution.py:46
  6.9 0.4 collective-permute-start.2
  7.2 0.1 collective-permute-start.6
  7.4 0.7 shard_map.39
  8.2 0.4 collective-permute-start.5
  8.6 0.2 collective-permute-start.8
  8.7 0.8 %collective-permute-done.5.refs_0_ = f32[32,896]{1,0:T(8,128)S(1)} collective-permute-done((f32[32,896]{1,0:T(8,128)S(1)}, f32[32,896]{1,0:T(8,128)S(1)}, u32[]{:S(2)}, u32[]{:S(2)}) %collective-permute-start.5) | collective-permute-done | bytes 114720 | tf_op jit(solution)/shard_map/ppermute | solution.py:35
  9.5 0.4 collective-permute-start.7
  9.9 0.2 collective-permute-start.10
  10.1 0.8 %collective-permute-done.7.refs_0_ = f32[32,896]{1,0:T(8,128)S(1)} collective-permute-done((f32[32,896]{1,0:T(8,128)S(1)}, f32[32,896]{1,0:T(8,128)S(1)}, u32[]{:S(2)}, u32[]{:S(2)}) %collective-permute-start.7) | collective-permute-done | bytes 114720 | tf_op jit(solution)/shard_map/ppermute | solution.py:35
  10.9 0.4 collective-permute-start.9
  11.2 0.2 collective-permute-start.12
  11.4 0.8 %collective-permute-done.9.refs_0_ = f32[32,896]{1,0:T(8,128)S(1)} collective-permute-done((f32[32,896]{1,0:T(8,128)S(1)}, f32[32,896]{1,0:T(8,128)S(1)}, u32[]{:S(2)}, u32[]{:S(2)}) %collective-permute-start.9) | collective-permute-done | bytes 114720 | tf_op jit(solution)/shard_map/ppermute | solution.py:35
  12.2 0.4 collective-permute-start.11
  12.6 0.2 collective-permute-start.14
  12.7 0.8 %collective-permute-done.11.refs_0_ = f32[32,896]{1,0:T(8,128)S(1)} collective-permute-done((f32[32,896]{1,0:T(8,128)S(1)}, f32[32,896]{1,0:T(8,128)S(1)}, u32[]{:S(2)}, u32[]{:S(2)}) %collective-permute-start.11) | collective-permute-done | bytes 114720 | tf_op jit(solution)/shard_map/ppermute | solution.py:35
  13.5 0.4 collective-permute-start.13
  13.9 0.2 collective-permute-start.16
  14.0 0.8 %collective-permute-done.13.refs_0_ = f32[32,896]{1,0:T(8,128)S(1)} collective-permute-done((f32[32,896]{1,0:T(8,128)S(1)}, f32[32,896]{1,0:T(8,128)S(1)}, u32[]{:S(2)}, u32[]{:S(2)}) %collective-permute-start.13) | collective-permute-done | bytes 114720 | tf_op jit(solution)/shard_map/ppermute | solution.py:35
  14.8 0.4 collective-permute-done.16.refs_0_
  15.2 25.4 %collective-permute-done.18.refs_0_ = f32[448,896]{1,0:T(8,128)S(1)} collective-permute-done((f32[448,896]{1,0:T(8,128)S(1)}, f32[448,896]{1,0:T(8,128)S(1)}, u32[]{:S(2)}, u32[]{:S(2)}) %collective-permute-start.18) | collective-permute-done | bytes 1605664 | tf_op jit(solution)/shard_map/ppermute | solution.py:39
  40.6 0.9 %collective-permute-start.19 = (f32[448,896]{1,0:T(8,128)S(1)}, f32[448,896]{1,0:T(8,128)S(1)}, u32[]{:S(2)}, u32[]{:S(2)}) collective-permute-start(f32[448,896]{1,0:T(8,128)S(1)} %gate.1.own_ref), channel_id=1, source_target_pairs={{0,1},{1,0},{2,3},{3,2},{4,5},{5,4},{6,7},{7,6},{8,9},{9,8},{10,11... | collective-permute-start | bytes 4816904 | tf_op jit(solution)/shard_map/ppermute | solution.py:46
  41.5 1.3 %collective-permute-start.20 = (f32[64,896]{1,0:T(8,128)S(1)}, f32[64,896]{1,0:T(8,128)S(1)}, u32[]{:S(2)}, u32[]{:S(2)}) collective-permute-start(f32[64,896]{1,0:T(8,128)S(1)} %get-tuple-element.15.refs_3_.refs_4_), channel_id=1, source_target_pairs={{16,18},{17,19},{20,22},{21,23},{24,26},{25,27},{28,30},{29,31}} | collective-permute-start | bytes 688136 | tf_op jit(solution)/shard_map/ppermute | solution.py:39
  42.8 0.6 collective-permute-start.21
  43.4 1.4 %collective-permute-done.15.refs_0_ = f32[32,896]{1,0:T(8,128)S(1)} collective-permute-done((f32[32,896]{1,0:T(8,128)S(1)}, f32[32,896]{1,0:T(8,128)S(1)}, u32[]{:S(2)}, u32[]{:S(2)}) %collective-permute-start.15) | collective-permute-done | bytes 114720 | tf_op jit(solution)/shard_map/ppermute | solution.py:35
  44.7 0.4 collective-permute-start.17
  45.1 0.2 collective-permute-start.23
  45.3 0.5 shard_map.53.refs_4_.refs_5_
  45.8 4.2 %collective-permute-done.20.refs_5_.refs_6_ = f32[64,896]{1,0:T(8,128)S(1)} collective-permute-done((f32[64,896]{1,0:T(8,128)S(1)}, f32[64,896]{1,0:T(8,128)S(1)}, u32[]{:S(2)}, u32[]{:S(2)}) %collective-permute-start.20) | collective-permute-done | bytes 229408 | tf_op jit(solution)/shard_map/ppermute | solution.py:39
  50.0 1.4 %collective-permute-start.22 = (f32[32,896]{1,0:T(8,128)S(1)}, f32[32,896]{1,0:T(8,128)S(1)}, u32[]{:S(2)}, u32[]{:S(2)}) collective-permute-start(f32[32,896]{1,0:T(8,128)S(1)} %shard_map.55.refs_6_.refs_1_), channel_id=1, source_target_pairs={{0,1},{1,0},{2,3},{3,2},{4,5},{5,4},{6,7},{7,6},{8,9},{9,8},{10,11... | collective-permute-start | bytes 344072 | tf_op jit(solution)/shard_map/ppermute | solution.py:35
  51.5 0.9 %collective-permute-done.22.refs_0_ = f32[32,896]{1,0:T(8,128)S(1)} collective-permute-done((f32[32,896]{1,0:T(8,128)S(1)}, f32[32,896]{1,0:T(8,128)S(1)}, u32[]{:S(2)}, u32[]{:S(2)}) %collective-permute-start.22) | collective-permute-done | bytes 114720 | tf_op jit(solution)/shard_map/ppermute | solution.py:35
  52.4 4.4 %collective-permute-start.24 = (f32[32,896]{1,0:T(8,128)S(1)}, f32[32,896]{1,0:T(8,128)S(1)}, u32[]{:S(2)}, u32[]{:S(2)}) collective-permute-start(f32[32,896]{1,0:T(8,128)S(1)} %shard_map.57.refs_6_.refs_1_), channel_id=1, source_target_pairs={{0,1},{1,0},{2,3},{3,2},{4,5},{5,4},{6,7},{7,6},{8,9},{9,8},{10,11... | collective-permute-start | bytes 344072 | tf_op jit(solution)/shard_map/ppermute | solution.py:35
  56.8 2.8 %collective-permute-start.28 = (f32[32,896]{1,0:T(8,128)S(1)}, f32[32,896]{1,0:T(8,128)S(1)}, u32[]{:S(2)}, u32[]{:S(2)}) collective-permute-start(f32[32,896]{1,0:T(8,128)S(1)} %shard_map.58.refs_6_.refs_1_), channel_id=1, source_target_pairs={{0,1},{1,0},{2,3},{3,2},{4,5},{5,4},{6,7},{7,6},{8,9},{9,8},{10,11... | collective-permute-start | bytes 344072 | tf_op jit(solution)/shard_map/ppermute | solution.py:35
  59.7 0.7 shard_map.59.refs_6_.refs_2_
  60.5 2.3 %collective-permute-done.28.refs_0_ = f32[32,896]{1,0:T(8,128)S(1)} collective-permute-done((f32[32,896]{1,0:T(8,128)S(1)}, f32[32,896]{1,0:T(8,128)S(1)}, u32[]{:S(2)}, u32[]{:S(2)}) %collective-permute-start.28) | collective-permute-done | bytes 114720 | tf_op jit(solution)/shard_map/ppermute | solution.py:35
  62.8 0.7 shard_map.60.refs_7_.refs_2_
  63.5 3.3 %collective-permute-start.29 = (f32[32,896]{1,0:T(8,128)S(1)}, f32[32,896]{1,0:T(8,128)S(1)}, u32[]{:S(2)}, u32[]{:S(2)}) collective-permute-start(f32[32,896]{1,0:T(8,128)S(1)} %shard_map.60.refs_7_.refs_2_), channel_id=1, source_target_pairs={{0,1},{1,0},{2,3},{3,2},{4,5},{5,4},{6,7},{7,6},{8,9},{9,8},{10,11... | collective-permute-start | bytes 344072 | tf_op jit(solution)/shard_map/ppermute | solution.py:35
  66.8 1.0 %collective-permute-start.30 = (f32[32,896]{1,0:T(8,128)S(1)}, f32[32,896]{1,0:T(8,128)S(1)}, u32[]{:S(2)}, u32[]{:S(2)}) collective-permute-start(f32[32,896]{1,0:T(8,128)S(1)} %shard_map.60.refs_7_.refs_2_), channel_id=1, source_target_pairs={{0,1},{1,0},{2,3},{3,2},{4,5},{5,4},{6,7},{7,6},{8,9},{9,8},{10,11... | collective-permute-start | bytes 344072 | tf_op jit(solution)/shard_map/ppermute | solution.py:35
  67.8 6.2 %collective-permute-done.29.refs_0_ = f32[32,896]{1,0:T(8,128)S(1)} collective-permute-done((f32[32,896]{1,0:T(8,128)S(1)}, f32[32,896]{1,0:T(8,128)S(1)}, u32[]{:S(2)}, u32[]{:S(2)}) %collective-permute-start.29) | collective-permute-done | bytes 114720 | tf_op jit(solution)/shard_map/ppermute | solution.py:35
  74.0 0.2 shard_map.63
  74.2 1.9 %collective-permute-start.31 = (f32[64,448]{1,0:T(8,128)S(1)}, f32[64,448]{1,0:T(8,128)S(1)}, u32[]{:S(2)}, u32[]{:S(2)}) collective-permute-start(f32[64,448]{1,0:T(8,128)S(1)} %shard_map.63), channel_id=1, source_target_pairs={{0,1},{1,0},{2,3},{3,2},{4,5},{5,4},{6,7},{7,6},{8,9},{9,8},{10,11... | collective-permute-start | bytes 344072 | tf_op jit(solution)/shard_map/ppermute | solution.py:46
  76.1 1.0 %collective-permute-done.31.refs_2_ = f32[64,448]{1,0:T(8,128)S(1)} collective-permute-done((f32[64,448]{1,0:T(8,128)S(1)}, f32[64,448]{1,0:T(8,128)S(1)}, u32[]{:S(2)}, u32[]{:S(2)}) %collective-permute-start.31) | collective-permute-done | bytes 114720 | tf_op jit(solution)/shard_map/ppermute | solution.py:46
  77.1 0.9 %shard_map.64 = f32[448,128]{1,0:T(8,128)} custom-call(f32[32,896]{1,0:T(8,128)S(1)} %shard_map.61.refs_7_.refs_0_, f32[32,896]{1,0:T(8,128)S(1)} %shard_map.62.refs_1_, f32[64,448]{1,0:T(8,128)S(1)} %collective-permute-done.31.refs_2_), custom_call_target="tpu_custom_call" | custom-call | bytes 229376 | tf_op jit(solution)/shard_map/pallas_call | solution.py:51
  (52 shorter events, 0.6 us)
Async XLA Ops:
  0.0 5.5 %copy-start = (bf16[1,448,896]{2,1,0:T(8,128)(2,1)S(1)}, bf16[1,448,896]{2,1,0:T(8,128)(2,1)}, u32[]{:S(2)}) copy-start(bf16[1,448,896]{2,1,0:T(8,128)(2,1)} %param.3) | copy-start | bytes 2408452
  0.0 3.4 %copy-start.2 = (f32[448,128]{1,0:T(8,128)S(1)}, f32[448,128]{1,0:T(8,128)}, u32[]{:S(2)}) copy-start(f32[448,128]{1,0:T(8,128)} %start_ref.1) | copy-start | bytes 688132
  0.0 5.5 %copy-start.1 = (f32[1,448,128]{2,1,0:T(8,128)S(1)}, f32[1,448,128]{2,1,0:T(8,128)}, u32[]{:S(2)}) copy-start(f32[1,448,128]{2,1,0:T(8,128)} %param.4) | copy-start | bytes 688132
  1.4 6.0 %collective-permute-start.3 = (f32[448,896]{1,0:T(8,128)S(1)}, f32[448,896]{1,0:T(8,128)S(1)}, u32[]{:S(2)}, u32[]{:S(2)}) collective-permute-start(f32[448,896]{1,0:T(8,128)S(1)} %bitcast_convert_fusion), channel_id=1, source_target_pairs={{0,1},{1,0},{2,3},{3,2},{4,5},{5,4},{6,7},{7,6},{8,9},{9,8},{10,11... | collective-permute-start | bytes 4816904 | tf_op jit(solution)/shard_map/ppermute | solution.py:46
  2.1 38.5 %collective-permute-start.18 = (f32[448,896]{1,0:T(8,128)S(1)}, f32[448,896]{1,0:T(8,128)S(1)}, u32[]{:S(2)}, u32[]{:S(2)}) collective-permute-start(f32[448,896]{1,0:T(8,128)S(1)} %bitcast_convert_fusion), channel_id=1, source_target_pairs={{16,18},{17,19},{20,22},{21,23},{24,26},{25,27},{28,30},{29,31}} | collective-permute-start | bytes 4816904 | tf_op jit(solution)/shard_map/ppermute | solution.py:39
  3.4 2.1 %collective-permute-start = (f32[448,128]{1,0:T(8,128)S(1)}, f32[448,128]{1,0:T(8,128)S(1)}, u32[]{:S(2)}, u32[]{:S(2)}) collective-permute-start(f32[448,128]{1,0:T(8,128)S(1)} %copy-done.2), channel_id=1, source_target_pairs={{0,1},{1,0},{2,3},{3,2},{4,5},{5,4},{6,7},{7,6},{8,9},{9,8},{10,11... | collective-permute-start | bytes 688136 | tf_op jit(solution)/shard_map/ppermute | solution.py:46
  5.5 1.4 %collective-permute-start.1 = (f32[64,448]{1,0:T(8,128)S(1)}, f32[64,448]{1,0:T(8,128)S(1)}, u32[]{:S(2)}, u32[]{:S(2)}) collective-permute-start(f32[64,448]{1,0:T(8,128)S(1)} %get-tuple-element.12), channel_id=1, source_target_pairs={{0,1},{1,0},{2,3},{3,2},{4,5},{5,4},{6,7},{7,6},{8,9},{9,8},{10,11... | collective-permute-start | bytes 344072 | tf_op jit(solution)/shard_map/ppermute | solution.py:46
  5.9 1.5 %collective-permute-start.4 = (f32[448,128]{1,0:T(8,128)S(1)}, f32[448,128]{1,0:T(8,128)S(1)}, u32[]{:S(2)}, u32[]{:S(2)}) collective-permute-start(f32[448,128]{1,0:T(8,128)S(1)} %bitcast.7), channel_id=1, source_target_pairs={{0,1},{1,0},{2,3},{3,2},{4,5},{5,4},{6,7},{7,6},{8,9},{9,8},{10,11... | collective-permute-start | bytes 688136 | tf_op jit(solution)/shard_map/ppermute | solution.py:46
  6.9 1.3 %collective-permute-start.2 = (f32[32,896]{1,0:T(8,128)S(1)}, f32[32,896]{1,0:T(8,128)S(1)}, u32[]{:S(2)}, u32[]{:S(2)}) collective-permute-start(f32[32,896]{1,0:T(8,128)S(1)} %get-tuple-element.13.refs_1_), channel_id=1, source_target_pairs={{0,2},{1,3},{2,0},{3,1},{4,5},{5,4},{6,7},{7,6},{8,9},{9,8},{10,11... | collective-permute-start | bytes 344072 | tf_op jit(solution)/shard_map/ppermute | solution.py:35
  7.2 1.3 %collective-permute-start.6 = (f32[32,896]{1,0:T(8,128)S(1)}, f32[32,896]{1,0:T(8,128)S(1)}, u32[]{:S(2)}, u32[]{:S(2)}) collective-permute-start(f32[32,896]{1,0:T(8,128)S(1)} %get-tuple-element.16.refs_4_.refs_1_), channel_id=1, source_target_pairs={{0,2},{1,3},{2,0},{3,1},{4,5},{5,4},{6,7},{7,6},{8,9},{9,8},{10,11... | collective-permute-start | bytes 344072 | tf_op jit(solution)/shard_map/ppermute | solution.py:35
  8.2 1.3 %collective-permute-start.5 = (f32[32,896]{1,0:T(8,128)S(1)}, f32[32,896]{1,0:T(8,128)S(1)}, u32[]{:S(2)}, u32[]{:S(2)}) collective-permute-start(f32[32,896]{1,0:T(8,128)S(1)} %shard_map.40.refs_4_.refs_1_), channel_id=1, source_target_pairs={{0,1},{1,0},{2,4},{3,5},{4,2},{5,3},{6,7},{7,6},{8,9},{9,8},{10,11... | collective-permute-start | bytes 344072 | tf_op jit(solution)/shard_map/ppermute | solution.py:35
  8.6 1.3 %collective-permute-start.8 = (f32[32,896]{1,0:T(8,128)S(1)}, f32[32,896]{1,0:T(8,128)S(1)}, u32[]{:S(2)}, u32[]{:S(2)}) collective-permute-start(f32[32,896]{1,0:T(8,128)S(1)} %shard_map.41.refs_4_.refs_1_), channel_id=1, source_target_pairs={{0,1},{1,0},{2,4},{3,5},{4,2},{5,3},{6,7},{7,6},{8,9},{9,8},{10,11... | collective-permute-start | bytes 344072 | tf_op jit(solution)/shard_map/ppermute | solution.py:35
  9.5 1.3 %collective-permute-start.7 = (f32[32,896]{1,0:T(8,128)S(1)}, f32[32,896]{1,0:T(8,128)S(1)}, u32[]{:S(2)}, u32[]{:S(2)}) collective-permute-start(f32[32,896]{1,0:T(8,128)S(1)} %shard_map.42.refs_4_.refs_1_), channel_id=1, source_target_pairs={{0,1},{1,0},{2,3},{3,2},{4,6},{5,7},{6,4},{7,5},{8,9},{9,8},{10,11... | collective-permute-start | bytes 344072 | tf_op jit(solution)/shard_map/ppermute | solution.py:35
  9.9 1.3 %collective-permute-start.10 = (f32[32,896]{1,0:T(8,128)S(1)}, f32[32,896]{1,0:T(8,128)S(1)}, u32[]{:S(2)}, u32[]{:S(2)}) collective-permute-start(f32[32,896]{1,0:T(8,128)S(1)} %shard_map.43.refs_4_.refs_1_), channel_id=1, source_target_pairs={{0,1},{1,0},{2,3},{3,2},{4,6},{5,7},{6,4},{7,5},{8,9},{9,8},{10,11... | collective-permute-start | bytes 344072 | tf_op jit(solution)/shard_map/ppermute | solution.py:35
  10.9 1.3 %collective-permute-start.9 = (f32[32,896]{1,0:T(8,128)S(1)}, f32[32,896]{1,0:T(8,128)S(1)}, u32[]{:S(2)}, u32[]{:S(2)}) collective-permute-start(f32[32,896]{1,0:T(8,128)S(1)} %shard_map.44.refs_4_.refs_1_), channel_id=1, source_target_pairs={{0,1},{1,0},{2,3},{3,2},{4,5},{5,4},{6,8},{7,9},{8,6},{9,7},{10,11... | collective-permute-start | bytes 344072 | tf_op jit(solution)/shard_map/ppermute | solution.py:35
  11.2 1.3 %collective-permute-start.12 = (f32[32,896]{1,0:T(8,128)S(1)}, f32[32,896]{1,0:T(8,128)S(1)}, u32[]{:S(2)}, u32[]{:S(2)}) collective-permute-start(f32[32,896]{1,0:T(8,128)S(1)} %shard_map.45.refs_4_.refs_1_), channel_id=1, source_target_pairs={{0,1},{1,0},{2,3},{3,2},{4,5},{5,4},{6,8},{7,9},{8,6},{9,7},{10,11... | collective-permute-start | bytes 344072 | tf_op jit(solution)/shard_map/ppermute | solution.py:35
  12.2 1.3 %collective-permute-start.11 = (f32[32,896]{1,0:T(8,128)S(1)}, f32[32,896]{1,0:T(8,128)S(1)}, u32[]{:S(2)}, u32[]{:S(2)}) collective-permute-start(f32[32,896]{1,0:T(8,128)S(1)} %shard_map.46.refs_4_.refs_1_), channel_id=1, source_target_pairs={{0,1},{1,0},{2,3},{3,2},{4,5},{5,4},{6,7},{7,6},{8,10},{9,11},{10,... | collective-permute-start | bytes 344072 | tf_op jit(solution)/shard_map/ppermute | solution.py:35
  12.6 1.3 %collective-permute-start.14 = (f32[32,896]{1,0:T(8,128)S(1)}, f32[32,896]{1,0:T(8,128)S(1)}, u32[]{:S(2)}, u32[]{:S(2)}) collective-permute-start(f32[32,896]{1,0:T(8,128)S(1)} %shard_map.47.refs_4_.refs_1_), channel_id=1, source_target_pairs={{0,1},{1,0},{2,3},{3,2},{4,5},{5,4},{6,7},{7,6},{8,10},{9,11},{10,... | collective-permute-start | bytes 344072 | tf_op jit(solution)/shard_map/ppermute | solution.py:35
  13.5 1.3 %collective-permute-start.13 = (f32[32,896]{1,0:T(8,128)S(1)}, f32[32,896]{1,0:T(8,128)S(1)}, u32[]{:S(2)}, u32[]{:S(2)}) collective-permute-start(f32[32,896]{1,0:T(8,128)S(1)} %shard_map.48.refs_4_.refs_1_), channel_id=1, source_target_pairs={{0,1},{1,0},{2,3},{3,2},{4,5},{5,4},{6,7},{7,6},{8,9},{9,8},{10,12... | collective-permute-start | bytes 344072 | tf_op jit(solution)/shard_map/ppermute | solution.py:35
  13.9 1.3 %collective-permute-start.16 = (f32[32,896]{1,0:T(8,128)S(1)}, f32[32,896]{1,0:T(8,128)S(1)}, u32[]{:S(2)}, u32[]{:S(2)}) collective-permute-start(f32[32,896]{1,0:T(8,128)S(1)} %shard_map.49.refs_4_.refs_1_), channel_id=1, source_target_pairs={{0,1},{1,0},{2,3},{3,2},{4,5},{5,4},{6,7},{7,6},{8,9},{9,8},{10,12... | collective-permute-start | bytes 344072 | tf_op jit(solution)/shard_map/ppermute | solution.py:35
  40.6 4.7 %collective-permute-start.19 = (f32[448,896]{1,0:T(8,128)S(1)}, f32[448,896]{1,0:T(8,128)S(1)}, u32[]{:S(2)}, u32[]{:S(2)}) collective-permute-start(f32[448,896]{1,0:T(8,128)S(1)} %gate.1.own_ref), channel_id=1, source_target_pairs={{0,1},{1,0},{2,3},{3,2},{4,5},{5,4},{6,7},{7,6},{8,9},{9,8},{10,11... | collective-permute-start | bytes 4816904 | tf_op jit(solution)/shard_map/ppermute | solution.py:46
  41.5 3.2 %collective-permute-start.15 = (f32[32,896]{1,0:T(8,128)S(1)}, f32[32,896]{1,0:T(8,128)S(1)}, u32[]{:S(2)}, u32[]{:S(2)}) collective-permute-start(f32[32,896]{1,0:T(8,128)S(1)} %shard_map.50.refs_4_.refs_1_), channel_id=1, source_target_pairs={{0,1},{1,0},{2,3},{3,2},{4,5},{5,4},{6,7},{7,6},{8,9},{9,8},{10,11... | collective-permute-start | bytes 344072 | tf_op jit(solution)/shard_map/ppermute | solution.py:35
  41.5 8.5 %collective-permute-start.20 = (f32[64,896]{1,0:T(8,128)S(1)}, f32[64,896]{1,0:T(8,128)S(1)}, u32[]{:S(2)}, u32[]{:S(2)}) collective-permute-start(f32[64,896]{1,0:T(8,128)S(1)} %get-tuple-element.15.refs_3_.refs_4_), channel_id=1, source_target_pairs={{16,18},{17,19},{20,22},{21,23},{24,26},{25,27},{28,30},{29,31}} | collective-permute-start | bytes 688136 | tf_op jit(solution)/shard_map/ppermute | solution.py:39
  42.8 2.3 %collective-permute-start.21 = (f32[32,896]{1,0:T(8,128)S(1)}, f32[32,896]{1,0:T(8,128)S(1)}, u32[]{:S(2)}, u32[]{:S(2)}) collective-permute-start(f32[32,896]{1,0:T(8,128)S(1)} %shard_map.51.refs_4_.refs_2_.refs_1_), channel_id=1, source_target_pairs={{0,1},{1,0},{2,3},{3,2},{4,5},{5,4},{6,7},{7,6},{8,9},{9,8},{10,11... | collective-permute-start | bytes 344072 | tf_op jit(solution)/shard_map/ppermute | solution.py:35
  44.7 5.3 %collective-permute-start.17 = (f32[32,896]{1,0:T(8,128)S(1)}, f32[32,896]{1,0:T(8,128)S(1)}, u32[]{:S(2)}, u32[]{:S(2)}) collective-permute-start(f32[32,896]{1,0:T(8,128)S(1)} %shard_map.52.refs_4_.refs_1_), channel_id=1, source_target_pairs={{0,1},{1,0},{2,3},{3,2},{4,5},{5,4},{6,7},{7,6},{8,9},{9,8},{10,11... | collective-permute-start | bytes 344072 | tf_op jit(solution)/shard_map/ppermute | solution.py:35
  45.1 6.3 %collective-permute-start.23 = (f32[32,896]{1,0:T(8,128)S(1)}, f32[32,896]{1,0:T(8,128)S(1)}, u32[]{:S(2)}, u32[]{:S(2)}) collective-permute-start(f32[32,896]{1,0:T(8,128)S(1)} %shard_map.54.refs_6_.refs_1_), channel_id=1, source_target_pairs={{0,1},{1,0},{2,3},{3,2},{4,5},{5,4},{6,7},{7,6},{8,9},{9,8},{10,11... | collective-permute-start | bytes 344072 | tf_op jit(solution)/shard_map/ppermute | solution.py:35
  50.0 2.3 %collective-permute-start.22 = (f32[32,896]{1,0:T(8,128)S(1)}, f32[32,896]{1,0:T(8,128)S(1)}, u32[]{:S(2)}, u32[]{:S(2)}) collective-permute-start(f32[32,896]{1,0:T(8,128)S(1)} %shard_map.55.refs_6_.refs_1_), channel_id=1, source_target_pairs={{0,1},{1,0},{2,3},{3,2},{4,5},{5,4},{6,7},{7,6},{8,9},{9,8},{10,11... | collective-permute-start | bytes 344072 | tf_op jit(solution)/shard_map/ppermute | solution.py:35
  51.4 5.4 %collective-permute-start.25 = (f32[32,896]{1,0:T(8,128)S(1)}, f32[32,896]{1,0:T(8,128)S(1)}, u32[]{:S(2)}, u32[]{:S(2)}) collective-permute-start(f32[32,896]{1,0:T(8,128)S(1)} %shard_map.56.refs_6_.refs_1_), channel_id=1, source_target_pairs={{0,1},{1,0},{2,3},{3,2},{4,5},{5,4},{6,7},{7,6},{8,9},{9,8},{10,11... | collective-permute-start | bytes 344072 | tf_op jit(solution)/shard_map/ppermute | solution.py:35
  52.4 7.3 %collective-permute-start.24 = (f32[32,896]{1,0:T(8,128)S(1)}, f32[32,896]{1,0:T(8,128)S(1)}, u32[]{:S(2)}, u32[]{:S(2)}) collective-permute-start(f32[32,896]{1,0:T(8,128)S(1)} %shard_map.57.refs_6_.refs_1_), channel_id=1, source_target_pairs={{0,1},{1,0},{2,3},{3,2},{4,5},{5,4},{6,7},{7,6},{8,9},{9,8},{10,11... | collective-permute-start | bytes 344072 | tf_op jit(solution)/shard_map/ppermute | solution.py:35
  56.8 6.0 %collective-permute-start.28 = (f32[32,896]{1,0:T(8,128)S(1)}, f32[32,896]{1,0:T(8,128)S(1)}, u32[]{:S(2)}, u32[]{:S(2)}) collective-permute-start(f32[32,896]{1,0:T(8,128)S(1)} %shard_map.58.refs_6_.refs_1_), channel_id=1, source_target_pairs={{0,1},{1,0},{2,3},{3,2},{4,5},{5,4},{6,7},{7,6},{8,9},{9,8},{10,11... | collective-permute-start | bytes 344072 | tf_op jit(solution)/shard_map/ppermute | solution.py:35
  60.4 7.4 %collective-permute-start.26 = (f32[32,896]{1,0:T(8,128)S(1)}, f32[32,896]{1,0:T(8,128)S(1)}, u32[]{:S(2)}, u32[]{:S(2)}) collective-permute-start(f32[32,896]{1,0:T(8,128)S(1)} %shard_map.59.refs_6_.refs_2_), channel_id=1, source_target_pairs={{0,1},{1,0},{2,3},{3,2},{4,5},{5,4},{6,7},{7,6},{8,9},{9,8},{10,11... | collective-permute-start | bytes 344072 | tf_op jit(solution)/shard_map/ppermute | solution.py:35
  60.4 7.4 %collective-permute-start.27 = (f32[32,896]{1,0:T(8,128)S(1)}, f32[32,896]{1,0:T(8,128)S(1)}, u32[]{:S(2)}, u32[]{:S(2)}) collective-permute-start(f32[32,896]{1,0:T(8,128)S(1)} %shard_map.59.refs_6_.refs_2_), channel_id=1, source_target_pairs={{0,1},{1,0},{2,3},{3,2},{4,5},{5,4},{6,7},{7,6},{8,9},{9,8},{10,11... | collective-permute-start | bytes 344072 | tf_op jit(solution)/shard_map/ppermute | solution.py:35
  63.5 10.5 %collective-permute-start.29 = (f32[32,896]{1,0:T(8,128)S(1)}, f32[32,896]{1,0:T(8,128)S(1)}, u32[]{:S(2)}, u32[]{:S(2)}) collective-permute-start(f32[32,896]{1,0:T(8,128)S(1)} %shard_map.60.refs_7_.refs_2_), channel_id=1, source_target_pairs={{0,1},{1,0},{2,3},{3,2},{4,5},{5,4},{6,7},{7,6},{8,9},{9,8},{10,11... | collective-permute-start | bytes 344072 | tf_op jit(solution)/shard_map/ppermute | solution.py:35
  66.8 7.2 %collective-permute-start.30 = (f32[32,896]{1,0:T(8,128)S(1)}, f32[32,896]{1,0:T(8,128)S(1)}, u32[]{:S(2)}, u32[]{:S(2)}) collective-permute-start(f32[32,896]{1,0:T(8,128)S(1)} %shard_map.60.refs_7_.refs_2_), channel_id=1, source_target_pairs={{0,1},{1,0},{2,3},{3,2},{4,5},{5,4},{6,7},{7,6},{8,9},{9,8},{10,11... | collective-permute-start | bytes 344072 | tf_op jit(solution)/shard_map/ppermute | solution.py:35
  74.2 2.9 %collective-permute-start.31 = (f32[64,448]{1,0:T(8,128)S(1)}, f32[64,448]{1,0:T(8,128)S(1)}, u32[]{:S(2)}, u32[]{:S(2)}) collective-permute-start(f32[64,448]{1,0:T(8,128)S(1)} %shard_map.63), channel_id=1, source_target_pairs={{0,1},{1,0},{2,3},{3,2},{4,5},{5,4},{6,7},{7,6},{8,9},{9,8},{10,11... | collective-permute-start | bytes 344072 | tf_op jit(solution)/shard_map/ppermute | solution.py:46

commit v2 on v1

--- a/solution.py
+++ b/solution.py
@@ -28,10 +28,10 @@
     return route
 
 
-def hop(block, pairs):
+def hop(block, *cycles):
     to = {}
-    for a, b in pairs:
-        to[a], to[b] = b, a
+    for cycle in cycles:
+        to.update(zip(cycle, cycle[1:] + cycle[:1]))
     return lax.ppermute(block, ("tm", "row"), route_of(to, True))
 
 
@@ -220,30 +220,30 @@
             aliases={count: 0} if alias else None, flops=product * (1 + double),
         )
 
-    def move(c, pairs):
-        return hop(ys[c], pairs)
+    def move(c, *cycles):
+        return hop(ys[c], *cycles)
 
     for stage in range(1, SINGLE):
-        if stage == SINGLE - 1:
-            shipped = gate(shipped, *ys)
-            shipped_other = swap_cores(shipped)
-            (moved,) = call(
-                functools.partial(migrate_kernel, odds), (shipped, shipped_other), [VMEM] * 2,
-                [shape((order, order), BF16)], limit=24,
-            )
         for c in range(CHUNKS):
-            x = move(c, [(stage - 1, stage)])
+            x = move(c, (stage - 1, stage))
             step(c, [x], {(0, False): [stage]})
+            if (stage, c) == (SINGLE - 1, 0):
+                shipped = gate(shipped, ys[c])
+                shipped_other = swap_cores(shipped)
+                (moved,) = call(
+                    functools.partial(migrate_kernel, odds), (shipped, shipped_other), [VMEM] * 2,
+                    [shape((order, order), BF16)], limit=24,
+                )
     for odd in odds:
         last = odd == slices - 1
-        pairs = [(odd - 2, odd)] + ([(odd - 4, odd - 3)] if odd > odds[0] else [])
+        cycles = [(odd - 2, odd, *([odd - 8] if odd == odds[0] else []))] + ([(odd - 4, odd - 3, odd - (5 if last else 11))] if odd > odds[0] else [])
         plan = {(0, True): [odd]}
         if odd > odds[0]:
             plan[(0, False)] = [odd - 3]
         if last:
             plan[(1, False)] = [odd - 1]
         for c in range(CHUNKS):
-            xs = [move(c, pairs)] + ([move(c, [(odd - 2, odd - 1)])] if last else [])
+            xs = [move(c, *cycles)] + ([move(c, (odd - 2, odd - 1, odd - 7))] if last else [])
             step(c, xs, plan, got=(moved, got_offset), alias=not last)
 
     def give_kernel(*refs):
@@ -261,9 +261,7 @@
         refs[-1][...] = rows.T
 
     (give,) = call(give_kernel, tuple(ys), [VMEM] * CHUNKS, [shape((half, part), F32)])
-    (out,) = call(
-        end_kernel, (*ys, swap_cores(give)), [VMEM] * (CHUNKS + 1), [shape((part, columns), F32)]
-    )
+    (out,) = call(end_kernel, (*ys, swap_cores(give)), [VMEM] * (CHUNKS + 1), [shape((part, columns), F32)])
     return out[None]
 
 

time: 78.1 us -> 77.2 us (0.988)
  the two profiles are of different devices: /device:TPU:27 before, /device:TPU:17 now
where the time goes in v2:
time: 77.2 us; the launch traced here: 77.1 us
  waiting for transfers between devices  41.8 us (54%)
  starting transfers between devices  31.2 us (40%)
  Pallas kernels  2.55 us (3%)
  other arithmetic  1.34 us (2%)
    ppermute x2, waiting for transfers between devices, ship(): lax.ppermute(block, ('tm', 'row'), route_of({e: e + 1 for e in evens}, Fa...  25.3 us
    ppermute x24, starting transfers between devices, hop(): return lax.ppermute(block, ('tm', 'row'), route_of(to, True))  20.4 us
    ppermute x24, waiting for transfers between devices, hop(): return lax.ppermute(block, ('tm', 'row'), route_of(to, True))  13.5 us
    ppermute x2, starting transfers between devices, ship(): lax.ppermute(block, ('tm', 'row'), route_of({e: e + 1 for e in evens}, Fa...  7.31 us
    ppermute x6, starting transfers between devices, swap_cores(): return lax.ppermute(block, ('tm', 'row'), route)  3.5 us
    ppermute x6, waiting for transfers between devices, swap_cores(): return lax.ppermute(block, ('tm', 'row'), route)  3.01 us
    pallas_call x28, Pallas kernels, call(): pl.pallas_call(kernel, out_shape=tuple(outs), in_specs=specs, out_specs=t...  2.55 us
  transfers between devices with their start and end apart: 32, of which 16 were waited for; matrix products, arithmetic and copies ran while one was open for 0% of the time, Pallas kernels for 2%

profile of v2, /device:TPU:17, one launch (start us, length us, event | category | flops | bytes accessed | tf_op | source)
XLA Modules:
  0.0 77.1 jit_solution(8051504103486449675)
XLA Ops:
  0.0 1.3 %bitcast_convert_fusion = f32[448,896]{1,0:T(8,128)S(1)} fusion(bf16[1,448,896]{2,1,0:T(8,128)(2,1)} %param.3), kind=kLoop, calls=%fused_computation | loop fusion | flops 401408 | bytes 2408448 | tf_op jit(solution)/shard_map/convert_element_type | solution.py:189
  1.4 0.7 collective-permute-start.3
  2.1 3.2 %collective-permute-start.18 = (f32[448,896]{1,0:T(8,128)S(1)}, f32[448,896]{1,0:T(8,128)S(1)}, u32[]{:S(2)}, u32[]{:S(2)}) collective-permute-start(f32[448,896]{1,0:T(8,128)S(1)} %bitcast_convert_fusion), channel_id=1, source_target_pairs={{16,18},{17,19},{20,22},{21,23},{24,26},{25,27},{28,30},{29,31}} | collective-permute-start | bytes 4816904 | tf_op jit(solution)/shard_map/ppermute | solution.py:39
  5.3 0.4 collective-permute-start
  5.7 1.2 %collective-permute-done.other_start_ref = f32[448,128]{1,0:T(8,128)S(1)} collective-permute-done((f32[448,128]{1,0:T(8,128)S(1)}, f32[448,128]{1,0:T(8,128)S(1)}, u32[]{:S(2)}, u32[]{:S(2)}) %collective-permute-start) | collective-permute-done | bytes 229408 | tf_op jit(solution)/shard_map/ppermute | solution.py:46
  6.9 0.3 collective-permute-start.1
  7.2 0.2 collective-permute-start.4
  7.4 0.8 %collective-permute-done.1.got_ref = f32[64,448]{1,0:T(8,128)S(1)} collective-permute-done((f32[64,448]{1,0:T(8,128)S(1)}, f32[64,448]{1,0:T(8,128)S(1)}, u32[]{:S(2)}, u32[]{:S(2)}) %collective-permute-start.1) | collective-permute-done | bytes 114720 | tf_op jit(solution)/shard_map/ppermute | solution.py:46
  8.2 0.3 collective-permute-start.2
  8.5 0.2 collective-permute-start.6
  8.8 0.7 shard_map.39
  9.6 0.3 collective-permute-start.5
  9.9 0.2 collective-permute-start.8
  10.1 0.8 %collective-permute-done.5.refs_0_ = f32[32,896]{1,0:T(8,128)S(1)} collective-permute-done((f32[32,896]{1,0:T(8,128)S(1)}, f32[32,896]{1,0:T(8,128)S(1)}, u32[]{:S(2)}, u32[]{:S(2)}) %collective-permute-start.5) | collective-permute-done | bytes 114720 | tf_op jit(solution)/shard_map/ppermute | solution.py:35
  10.9 0.3 collective-permute-start.7
  11.2 0.2 collective-permute-start.10
  11.4 0.8 %collective-permute-done.7.refs_0_ = f32[32,896]{1,0:T(8,128)S(1)} collective-permute-done((f32[32,896]{1,0:T(8,128)S(1)}, f32[32,896]{1,0:T(8,128)S(1)}, u32[]{:S(2)}, u32[]{:S(2)}) %collective-permute-start.7) | collective-permute-done | bytes 114720 | tf_op jit(solution)/shard_map/ppermute | solution.py:35
  12.2 0.3 collective-permute-start.9
  12.7 0.8 %collective-permute-done.9.refs_0_ = f32[32,896]{1,0:T(8,128)S(1)} collective-permute-done((f32[32,896]{1,0:T(8,128)S(1)}, f32[32,896]{1,0:T(8,128)S(1)}, u32[]{:S(2)}, u32[]{:S(2)}) %collective-permute-start.9) | collective-permute-done | bytes 114720 | tf_op jit(solution)/shard_map/ppermute | solution.py:35
  13.5 0.3 collective-permute-start.11
  13.8 0.2 collective-permute-start.14
  14.1 0.8 %collective-permute-done.11.refs_0_ = f32[32,896]{1,0:T(8,128)S(1)} collective-permute-done((f32[32,896]{1,0:T(8,128)S(1)}, f32[32,896]{1,0:T(8,128)S(1)}, u32[]{:S(2)}, u32[]{:S(2)}) %collective-permute-start.11) | collective-permute-done | bytes 114720 | tf_op jit(solution)/shard_map/ppermute | solution.py:35
  14.9 0.3 collective-permute-start.13
  15.2 0.2 collective-permute-start.16
  15.4 0.8 %collective-permute-done.13.refs_0_ = f32[32,896]{1,0:T(8,128)S(1)} collective-permute-done((f32[32,896]{1,0:T(8,128)S(1)}, f32[32,896]{1,0:T(8,128)S(1)}, u32[]{:S(2)}, u32[]{:S(2)}) %collective-permute-start.13) | collective-permute-done | bytes 114720 | tf_op jit(solution)/shard_map/ppermute | solution.py:35
  16.2 0.3 collective-permute-start.15
  16.5 1.0 %collective-permute-done.15.refs_0_ = f32[32,896]{1,0:T(8,128)S(1)} collective-permute-done((f32[32,896]{1,0:T(8,128)S(1)}, f32[32,896]{1,0:T(8,128)S(1)}, u32[]{:S(2)}, u32[]{:S(2)}) %collective-permute-start.15) | collective-permute-done | bytes 114720 | tf_op jit(solution)/shard_map/ppermute | solution.py:35
  17.5 22.1 %collective-permute-done.18.refs_0_ = f32[448,896]{1,0:T(8,128)S(1)} collective-permute-done((f32[448,896]{1,0:T(8,128)S(1)}, f32[448,896]{1,0:T(8,128)S(1)}, u32[]{:S(2)}, u32[]{:S(2)}) %collective-permute-start.18) | collective-permute-done | bytes 1605664 | tf_op jit(solution)/shard_map/ppermute | solution.py:39
  39.6 0.9 %collective-permute-start.19 = (f32[448,896]{1,0:T(8,128)S(1)}, f32[448,896]{1,0:T(8,128)S(1)}, u32[]{:S(2)}, u32[]{:S(2)}) collective-permute-start(f32[448,896]{1,0:T(8,128)S(1)} %gate.1.own_ref), channel_id=1, source_target_pairs={{0,1},{1,0},{2,3},{3,2},{4,5},{5,4},{6,7},{7,6},{8,9},{9,8},{10,11... | collective-permute-start | bytes 4816904 | tf_op jit(solution)/shard_map/ppermute | solution.py:46
  40.5 4.1 %collective-permute-start.20 = (f32[64,896]{1,0:T(8,128)S(1)}, f32[64,896]{1,0:T(8,128)S(1)}, u32[]{:S(2)}, u32[]{:S(2)}) collective-permute-start(f32[64,896]{1,0:T(8,128)S(1)} %get-tuple-element.15.refs_3_.refs_4_), channel_id=1, source_target_pairs={{16,18},{17,19},{20,22},{21,23},{24,26},{25,27},{28,30},{29,31}} | collective-permute-start | bytes 688136 | tf_op jit(solution)/shard_map/ppermute | solution.py:39
  44.6 0.3 collective-permute-start.21
  45.0 0.2 collective-permute-start.17
  45.2 0.8 %collective-permute-done.21.refs_0_ = f32[32,896]{1,0:T(8,128)S(1)} collective-permute-done((f32[32,896]{1,0:T(8,128)S(1)}, f32[32,896]{1,0:T(8,128)S(1)}, u32[]{:S(2)}, u32[]{:S(2)}) %collective-permute-start.21) | collective-permute-done | bytes 114720 | tf_op jit(solution)/shard_map/ppermute | solution.py:35
  46.0 0.3 collective-permute-start.23
  46.3 3.2 %collective-permute-done.20.refs_5_.refs_6_ = f32[64,896]{1,0:T(8,128)S(1)} collective-permute-done((f32[64,896]{1,0:T(8,128)S(1)}, f32[64,896]{1,0:T(8,128)S(1)}, u32[]{:S(2)}, u32[]{:S(2)}) %collective-permute-start.20) | collective-permute-done | bytes 229408 | tf_op jit(solution)/shard_map/ppermute | solution.py:39
  49.6 6.8 %collective-permute-start.25 = (f32[32,896]{1,0:T(8,128)S(1)}, f32[32,896]{1,0:T(8,128)S(1)}, u32[]{:S(2)}, u32[]{:S(2)}) collective-permute-start(f32[32,896]{1,0:T(8,128)S(1)} %shard_map.56.refs_6_.refs_1_), channel_id=1, source_target_pairs={{0,14},{1,15},{2,3},{3,2},{4,5},{5,4},{6,7},{7,6},{8,9},{9,8},{10,... | collective-permute-start | bytes 344072 | tf_op jit(solution)/shard_map/ppermute | solution.py:35
  56.4 2.5 %collective-permute-done.22.refs_0_ = f32[32,896]{1,0:T(8,128)S(1)} collective-permute-done((f32[32,896]{1,0:T(8,128)S(1)}, f32[32,896]{1,0:T(8,128)S(1)}, u32[]{:S(2)}, u32[]{:S(2)}) %collective-permute-start.22) | collective-permute-done | bytes 114720 | tf_op jit(solution)/shard_map/ppermute | solution.py:35
  58.9 0.4 shard_map.57.refs_6_.refs_1_
  59.2 1.8 %collective-permute-start.24 = (f32[32,896]{1,0:T(8,128)S(1)}, f32[32,896]{1,0:T(8,128)S(1)}, u32[]{:S(2)}, u32[]{:S(2)}) collective-permute-start(f32[32,896]{1,0:T(8,128)S(1)} %shard_map.57.refs_6_.refs_1_), channel_id=1, source_target_pairs={{0,1},{1,0},{2,3},{3,2},{4,18},{5,19},{6,7},{7,6},{8,9},{9,8},{10,... | collective-permute-start | bytes 344072 | tf_op jit(solution)/shard_map/ppermute | solution.py:35
  61.0 0.4 shard_map.58.refs_6_.refs_1_
  61.4 2.5 %collective-permute-start.28 = (f32[32,896]{1,0:T(8,128)S(1)}, f32[32,896]{1,0:T(8,128)S(1)}, u32[]{:S(2)}, u32[]{:S(2)}) collective-permute-start(f32[32,896]{1,0:T(8,128)S(1)} %shard_map.58.refs_6_.refs_1_), channel_id=1, source_target_pairs={{0,1},{1,0},{2,3},{3,2},{4,18},{5,19},{6,7},{7,6},{8,9},{9,8},{10,... | collective-permute-start | bytes 344072 | tf_op jit(solution)/shard_map/ppermute | solution.py:35
  64.0 0.8 %collective-permute-done.28.refs_0_ = f32[32,896]{1,0:T(8,128)S(1)} collective-permute-done((f32[32,896]{1,0:T(8,128)S(1)}, f32[32,896]{1,0:T(8,128)S(1)}, u32[]{:S(2)}, u32[]{:S(2)}) %collective-permute-start.28) | collective-permute-done | bytes 114720 | tf_op jit(solution)/shard_map/ppermute | solution.py:35
  64.9 3.6 %collective-permute-start.29 = (f32[32,896]{1,0:T(8,128)S(1)}, f32[32,896]{1,0:T(8,128)S(1)}, u32[]{:S(2)}, u32[]{:S(2)}) collective-permute-start(f32[32,896]{1,0:T(8,128)S(1)} %shard_map.60.refs_7_.refs_2_), channel_id=1, source_target_pairs={{0,1},{1,0},{2,3},{3,2},{4,5},{5,4},{6,7},{7,6},{8,9},{9,8},{10,11... | collective-permute-start | bytes 344072 | tf_op jit(solution)/shard_map/ppermute | solution.py:35
  68.5 1.4 %collective-permute-start.30 = (f32[32,896]{1,0:T(8,128)S(1)}, f32[32,896]{1,0:T(8,128)S(1)}, u32[]{:S(2)}, u32[]{:S(2)}) collective-permute-start(f32[32,896]{1,0:T(8,128)S(1)} %shard_map.60.refs_7_.refs_2_), channel_id=1, source_target_pairs={{0,1},{1,0},{2,3},{3,2},{4,5},{5,4},{6,7},{7,6},{8,9},{9,8},{10,11... | collective-permute-start | bytes 344072 | tf_op jit(solution)/shard_map/ppermute | solution.py:35
  69.9 4.1 %collective-permute-done.30.refs_1_ = f32[32,896]{1,0:T(8,128)S(1)} collective-permute-done((f32[32,896]{1,0:T(8,128)S(1)}, f32[32,896]{1,0:T(8,128)S(1)}, u32[]{:S(2)}, u32[]{:S(2)}) %collective-permute-start.30) | collective-permute-done | bytes 114720 | tf_op jit(solution)/shard_map/ppermute | solution.py:35
  74.2 1.0 %collective-permute-start.31 = (f32[64,448]{1,0:T(8,128)S(1)}, f32[64,448]{1,0:T(8,128)S(1)}, u32[]{:S(2)}, u32[]{:S(2)}) collective-permute-start(f32[64,448]{1,0:T(8,128)S(1)} %shard_map.63), channel_id=1, source_target_pairs={{0,1},{1,0},{2,3},{3,2},{4,5},{5,4},{6,7},{7,6},{8,9},{9,8},{10,11... | collective-permute-start | bytes 344072 | tf_op jit(solution)/shard_map/ppermute | solution.py:46
  75.2 1.0 %collective-permute-done.31.refs_2_ = f32[64,448]{1,0:T(8,128)S(1)} collective-permute-done((f32[64,448]{1,0:T(8,128)S(1)}, f32[64,448]{1,0:T(8,128)S(1)}, u32[]{:S(2)}, u32[]{:S(2)}) %collective-permute-start.31) | collective-permute-done | bytes 114720 | tf_op jit(solution)/shard_map/ppermute | solution.py:46
  76.2 0.9 %shard_map.64 = f32[448,128]{1,0:T(8,128)} custom-call(f32[32,896]{1,0:T(8,128)S(1)} %shard_map.61.refs_7_.refs_0_, f32[32,896]{1,0:T(8,128)S(1)} %shard_map.62.refs_1_, f32[64,448]{1,0:T(8,128)S(1)} %collective-permute-done.31.refs_2_), custom_call_target="tpu_custom_call" | custom-call | bytes 229376 | tf_op jit(solution)/shard_map/pallas_call | solution.py:51
  (52 shorter events, 0.7 us)
Async XLA Ops:
  0.0 6.9 %copy-start = (bf16[1,448,896]{2,1,0:T(8,128)(2,1)S(1)}, bf16[1,448,896]{2,1,0:T(8,128)(2,1)}, u32[]{:S(2)}) copy-start(bf16[1,448,896]{2,1,0:T(8,128)(2,1)} %param.3) | copy-start | bytes 2408452
  0.0 5.3 %copy-start.2 = (f32[448,128]{1,0:T(8,128)S(1)}, f32[448,128]{1,0:T(8,128)}, u32[]{:S(2)}) copy-start(f32[448,128]{1,0:T(8,128)} %start_ref.1) | copy-start | bytes 688132
  0.0 6.9 %copy-start.1 = (f32[1,448,128]{2,1,0:T(8,128)S(1)}, f32[1,448,128]{2,1,0:T(8,128)}, u32[]{:S(2)}) copy-start(f32[1,448,128]{2,1,0:T(8,128)} %param.4) | copy-start | bytes 688132
  1.4 7.4 %collective-permute-start.3 = (f32[448,896]{1,0:T(8,128)S(1)}, f32[448,896]{1,0:T(8,128)S(1)}, u32[]{:S(2)}, u32[]{:S(2)}) collective-permute-start(f32[448,896]{1,0:T(8,128)S(1)} %bitcast_convert_fusion), channel_id=1, source_target_pairs={{0,1},{1,0},{2,3},{3,2},{4,5},{5,4},{6,7},{7,6},{8,9},{9,8},{10,11... | collective-permute-start | bytes 4816904 | tf_op jit(solution)/shard_map/ppermute | solution.py:46
  2.1 37.5 %collective-permute-start.18 = (f32[448,896]{1,0:T(8,128)S(1)}, f32[448,896]{1,0:T(8,128)S(1)}, u32[]{:S(2)}, u32[]{:S(2)}) collective-permute-start(f32[448,896]{1,0:T(8,128)S(1)} %bitcast_convert_fusion), channel_id=1, source_target_pairs={{16,18},{17,19},{20,22},{21,23},{24,26},{25,27},{28,30},{29,31}} | collective-permute-start | bytes 4816904 | tf_op jit(solution)/shard_map/ppermute | solution.py:39
  5.3 1.6 %collective-permute-start = (f32[448,128]{1,0:T(8,128)S(1)}, f32[448,128]{1,0:T(8,128)S(1)}, u32[]{:S(2)}, u32[]{:S(2)}) collective-permute-start(f32[448,128]{1,0:T(8,128)S(1)} %copy-done.2), channel_id=1, source_target_pairs={{0,1},{1,0},{2,3},{3,2},{4,5},{5,4},{6,7},{7,6},{8,9},{9,8},{10,11... | collective-permute-start | bytes 688136 | tf_op jit(solution)/shard_map/ppermute | solution.py:46
  6.9 1.3 %collective-permute-start.1 = (f32[64,448]{1,0:T(8,128)S(1)}, f32[64,448]{1,0:T(8,128)S(1)}, u32[]{:S(2)}, u32[]{:S(2)}) collective-permute-start(f32[64,448]{1,0:T(8,128)S(1)} %get-tuple-element.12), channel_id=1, source_target_pairs={{0,1},{1,0},{2,3},{3,2},{4,5},{5,4},{6,7},{7,6},{8,9},{9,8},{10,11... | collective-permute-start | bytes 344072 | tf_op jit(solution)/shard_map/ppermute | solution.py:46
  7.2 1.6 %collective-permute-start.4 = (f32[448,128]{1,0:T(8,128)S(1)}, f32[448,128]{1,0:T(8,128)S(1)}, u32[]{:S(2)}, u32[]{:S(2)}) collective-permute-start(f32[448,128]{1,0:T(8,128)S(1)} %bitcast.7), channel_id=1, source_target_pairs={{0,1},{1,0},{2,3},{3,2},{4,5},{5,4},{6,7},{7,6},{8,9},{9,8},{10,11... | collective-permute-start | bytes 688136 | tf_op jit(solution)/shard_map/ppermute | solution.py:46
  8.2 1.3 %collective-permute-start.2 = (f32[32,896]{1,0:T(8,128)S(1)}, f32[32,896]{1,0:T(8,128)S(1)}, u32[]{:S(2)}, u32[]{:S(2)}) collective-permute-start(f32[32,896]{1,0:T(8,128)S(1)} %get-tuple-element.13.refs_1_), channel_id=1, source_target_pairs={{0,2},{1,3},{2,0},{3,1},{4,5},{5,4},{6,7},{7,6},{8,9},{9,8},{10,11... | collective-permute-start | bytes 344072 | tf_op jit(solution)/shard_map/ppermute | solution.py:35
  8.5 1.3 %collective-permute-start.6 = (f32[32,896]{1,0:T(8,128)S(1)}, f32[32,896]{1,0:T(8,128)S(1)}, u32[]{:S(2)}, u32[]{:S(2)}) collective-permute-start(f32[32,896]{1,0:T(8,128)S(1)} %get-tuple-element.16.refs_4_.refs_1_), channel_id=1, source_target_pairs={{0,2},{1,3},{2,0},{3,1},{4,5},{5,4},{6,7},{7,6},{8,9},{9,8},{10,11... | collective-permute-start | bytes 344072 | tf_op jit(solution)/shard_map/ppermute | solution.py:35
  9.6 1.3 %collective-permute-start.5 = (f32[32,896]{1,0:T(8,128)S(1)}, f32[32,896]{1,0:T(8,128)S(1)}, u32[]{:S(2)}, u32[]{:S(2)}) collective-permute-start(f32[32,896]{1,0:T(8,128)S(1)} %shard_map.40.refs_4_.refs_1_), channel_id=1, source_target_pairs={{0,1},{1,0},{2,4},{3,5},{4,2},{5,3},{6,7},{7,6},{8,9},{9,8},{10,11... | collective-permute-start | bytes 344072 | tf_op jit(solution)/shard_map/ppermute | solution.py:35
  9.9 1.3 %collective-permute-start.8 = (f32[32,896]{1,0:T(8,128)S(1)}, f32[32,896]{1,0:T(8,128)S(1)}, u32[]{:S(2)}, u32[]{:S(2)}) collective-permute-start(f32[32,896]{1,0:T(8,128)S(1)} %shard_map.41.refs_4_.refs_1_), channel_id=1, source_target_pairs={{0,1},{1,0},{2,4},{3,5},{4,2},{5,3},{6,7},{7,6},{8,9},{9,8},{10,11... | collective-permute-start | bytes 344072 | tf_op jit(solution)/shard_map/ppermute | solution.py:35
  10.9 1.3 %collective-permute-start.7 = (f32[32,896]{1,0:T(8,128)S(1)}, f32[32,896]{1,0:T(8,128)S(1)}, u32[]{:S(2)}, u32[]{:S(2)}) collective-permute-start(f32[32,896]{1,0:T(8,128)S(1)} %shard_map.42.refs_4_.refs_1_), channel_id=1, source_target_pairs={{0,1},{1,0},{2,3},{3,2},{4,6},{5,7},{6,4},{7,5},{8,9},{9,8},{10,11... | collective-permute-start | bytes 344072 | tf_op jit(solution)/shard_map/ppermute | solution.py:35
  11.2 1.3 %collective-permute-start.10 = (f32[32,896]{1,0:T(8,128)S(1)}, f32[32,896]{1,0:T(8,128)S(1)}, u32[]{:S(2)}, u32[]{:S(2)}) collective-permute-start(f32[32,896]{1,0:T(8,128)S(1)} %shard_map.43.refs_4_.refs_1_), channel_id=1, source_target_pairs={{0,1},{1,0},{2,3},{3,2},{4,6},{5,7},{6,4},{7,5},{8,9},{9,8},{10,11... | collective-permute-start | bytes 344072 | tf_op jit(solution)/shard_map/ppermute | solution.py:35
  12.2 1.3 %collective-permute-start.9 = (f32[32,896]{1,0:T(8,128)S(1)}, f32[32,896]{1,0:T(8,128)S(1)}, u32[]{:S(2)}, u32[]{:S(2)}) collective-permute-start(f32[32,896]{1,0:T(8,128)S(1)} %shard_map.44.refs_4_.refs_1_), channel_id=1, source_target_pairs={{0,1},{1,0},{2,3},{3,2},{4,5},{5,4},{6,8},{7,9},{8,6},{9,7},{10,11... | collective-permute-start | bytes 344072 | tf_op jit(solution)/shard_map/ppermute | solution.py:35
  12.5 1.3 %collective-permute-start.12 = (f32[32,896]{1,0:T(8,128)S(1)}, f32[32,896]{1,0:T(8,128)S(1)}, u32[]{:S(2)}, u32[]{:S(2)}) collective-permute-start(f32[32,896]{1,0:T(8,128)S(1)} %shard_map.45.refs_4_.refs_1_), channel_id=1, source_target_pairs={{0,1},{1,0},{2,3},{3,2},{4,5},{5,4},{6,8},{7,9},{8,6},{9,7},{10,11... | collective-permute-start | bytes 344072 | tf_op jit(solution)/shard_map/ppermute | solution.py:35
  13.5 1.3 %collective-permute-start.11 = (f32[32,896]{1,0:T(8,128)S(1)}, f32[32,896]{1,0:T(8,128)S(1)}, u32[]{:S(2)}, u32[]{:S(2)}) collective-permute-start(f32[32,896]{1,0:T(8,128)S(1)} %shard_map.46.refs_4_.refs_1_), channel_id=1, source_target_pairs={{0,1},{1,0},{2,3},{3,2},{4,5},{5,4},{6,7},{7,6},{8,10},{9,11},{10,... | collective-permute-start | bytes 344072 | tf_op jit(solution)/shard_map/ppermute | solution.py:35
  13.8 1.3 %collective-permute-start.14 = (f32[32,896]{1,0:T(8,128)S(1)}, f32[32,896]{1,0:T(8,128)S(1)}, u32[]{:S(2)}, u32[]{:S(2)}) collective-permute-start(f32[32,896]{1,0:T(8,128)S(1)} %shard_map.47.refs_4_.refs_1_), channel_id=1, source_target_pairs={{0,1},{1,0},{2,3},{3,2},{4,5},{5,4},{6,7},{7,6},{8,10},{9,11},{10,... | collective-permute-start | bytes 344072 | tf_op jit(solution)/shard_map/ppermute | solution.py:35
  14.9 1.3 %collective-permute-start.13 = (f32[32,896]{1,0:T(8,128)S(1)}, f32[32,896]{1,0:T(8,128)S(1)}, u32[]{:S(2)}, u32[]{:S(2)}) collective-permute-start(f32[32,896]{1,0:T(8,128)S(1)} %shard_map.48.refs_4_.refs_1_), channel_id=1, source_target_pairs={{0,1},{1,0},{2,3},{3,2},{4,5},{5,4},{6,7},{7,6},{8,9},{9,8},{10,12... | collective-permute-start | bytes 344072 | tf_op jit(solution)/shard_map/ppermute | solution.py:35
  15.2 1.3 %collective-permute-start.16 = (f32[32,896]{1,0:T(8,128)S(1)}, f32[32,896]{1,0:T(8,128)S(1)}, u32[]{:S(2)}, u32[]{:S(2)}) collective-permute-start(f32[32,896]{1,0:T(8,128)S(1)} %shard_map.49.refs_4_.refs_1_), channel_id=1, source_target_pairs={{0,1},{1,0},{2,3},{3,2},{4,5},{5,4},{6,7},{7,6},{8,9},{9,8},{10,12... | collective-permute-start | bytes 344072 | tf_op jit(solution)/shard_map/ppermute | solution.py:35
  16.2 1.3 %collective-permute-start.15 = (f32[32,896]{1,0:T(8,128)S(1)}, f32[32,896]{1,0:T(8,128)S(1)}, u32[]{:S(2)}, u32[]{:S(2)}) collective-permute-start(f32[32,896]{1,0:T(8,128)S(1)} %shard_map.50.refs_4_.refs_1_), channel_id=1, source_target_pairs={{0,1},{1,0},{2,3},{3,2},{4,5},{5,4},{6,7},{7,6},{8,9},{9,8},{10,11... | collective-permute-start | bytes 344072 | tf_op jit(solution)/shard_map/ppermute | solution.py:35
  39.6 6.7 %collective-permute-start.19 = (f32[448,896]{1,0:T(8,128)S(1)}, f32[448,896]{1,0:T(8,128)S(1)}, u32[]{:S(2)}, u32[]{:S(2)}) collective-permute-start(f32[448,896]{1,0:T(8,128)S(1)} %gate.1.own_ref), channel_id=1, source_target_pairs={{0,1},{1,0},{2,3},{3,2},{4,5},{5,4},{6,7},{7,6},{8,9},{9,8},{10,11... | collective-permute-start | bytes 4816904 | tf_op jit(solution)/shard_map/ppermute | solution.py:46
  40.5 9.0 %collective-permute-start.20 = (f32[64,896]{1,0:T(8,128)S(1)}, f32[64,896]{1,0:T(8,128)S(1)}, u32[]{:S(2)}, u32[]{:S(2)}) collective-permute-start(f32[64,896]{1,0:T(8,128)S(1)} %get-tuple-element.15.refs_3_.refs_4_), channel_id=1, source_target_pairs={{16,18},{17,19},{20,22},{21,23},{24,26},{25,27},{28,30},{29,31}} | collective-permute-start | bytes 688136 | tf_op jit(solution)/shard_map/ppermute | solution.py:39
  44.6 1.4 %collective-permute-start.21 = (f32[32,896]{1,0:T(8,128)S(1)}, f32[32,896]{1,0:T(8,128)S(1)}, u32[]{:S(2)}, u32[]{:S(2)}) collective-permute-start(f32[32,896]{1,0:T(8,128)S(1)} %shard_map.51.refs_4_.refs_1_), channel_id=1, source_target_pairs={{0,1},{1,0},{2,3},{3,2},{4,5},{5,4},{6,7},{7,6},{8,9},{9,8},{10,11... | collective-permute-start | bytes 344072 | tf_op jit(solution)/shard_map/ppermute | solution.py:35
  45.0 4.6 %collective-permute-start.17 = (f32[32,896]{1,0:T(8,128)S(1)}, f32[32,896]{1,0:T(8,128)S(1)}, u32[]{:S(2)}, u32[]{:S(2)}) collective-permute-start(f32[32,896]{1,0:T(8,128)S(1)} %shard_map.52.refs_1_.refs_4_), channel_id=1, source_target_pairs={{0,1},{1,0},{2,14},{3,15},{4,5},{5,4},{6,7},{7,6},{8,9},{9,8},{10,... | collective-permute-start | bytes 344072 | tf_op jit(solution)/shard_map/ppermute | solution.py:35
  46.0 3.5 %collective-permute-start.23 = (f32[32,896]{1,0:T(8,128)S(1)}, f32[32,896]{1,0:T(8,128)S(1)}, u32[]{:S(2)}, u32[]{:S(2)}) collective-permute-start(f32[32,896]{1,0:T(8,128)S(1)} %shard_map.54.refs_6_.refs_1_), channel_id=1, source_target_pairs={{0,1},{1,0},{2,14},{3,15},{4,5},{5,4},{6,7},{7,6},{8,9},{9,8},{10,... | collective-permute-start | bytes 344072 | tf_op jit(solution)/shard_map/ppermute | solution.py:35
  49.5 9.3 %collective-permute-start.22 = (f32[32,896]{1,0:T(8,128)S(1)}, f32[32,896]{1,0:T(8,128)S(1)}, u32[]{:S(2)}, u32[]{:S(2)}) collective-permute-start(f32[32,896]{1,0:T(8,128)S(1)} %shard_map.55.refs_6_.refs_1_), channel_id=1, source_target_pairs={{0,14},{1,15},{2,3},{3,2},{4,5},{5,4},{6,7},{7,6},{8,9},{9,8},{10,... | collective-permute-start | bytes 344072 | tf_op jit(solution)/shard_map/ppermute | solution.py:35
  49.6 11.5 %collective-permute-start.25 = (f32[32,896]{1,0:T(8,128)S(1)}, f32[32,896]{1,0:T(8,128)S(1)}, u32[]{:S(2)}, u32[]{:S(2)}) collective-permute-start(f32[32,896]{1,0:T(8,128)S(1)} %shard_map.56.refs_6_.refs_1_), channel_id=1, source_target_pairs={{0,14},{1,15},{2,3},{3,2},{4,5},{5,4},{6,7},{7,6},{8,9},{9,8},{10,... | collective-permute-start | bytes 344072 | tf_op jit(solution)/shard_map/ppermute | solution.py:35
  59.2 4.7 %collective-permute-start.24 = (f32[32,896]{1,0:T(8,128)S(1)}, f32[32,896]{1,0:T(8,128)S(1)}, u32[]{:S(2)}, u32[]{:S(2)}) collective-permute-start(f32[32,896]{1,0:T(8,128)S(1)} %shard_map.57.refs_6_.refs_1_), channel_id=1, source_target_pairs={{0,1},{1,0},{2,3},{3,2},{4,18},{5,19},{6,7},{7,6},{8,9},{9,8},{10,... | collective-permute-start | bytes 344072 | tf_op jit(solution)/shard_map/ppermute | solution.py:35
  61.4 3.5 %collective-permute-start.28 = (f32[32,896]{1,0:T(8,128)S(1)}, f32[32,896]{1,0:T(8,128)S(1)}, u32[]{:S(2)}, u32[]{:S(2)}) collective-permute-start(f32[32,896]{1,0:T(8,128)S(1)} %shard_map.58.refs_6_.refs_1_), channel_id=1, source_target_pairs={{0,1},{1,0},{2,3},{3,2},{4,18},{5,19},{6,7},{7,6},{8,9},{9,8},{10,... | collective-permute-start | bytes 344072 | tf_op jit(solution)/shard_map/ppermute | solution.py:35
  63.9 6.0 %collective-permute-start.26 = (f32[32,896]{1,0:T(8,128)S(1)}, f32[32,896]{1,0:T(8,128)S(1)}, u32[]{:S(2)}, u32[]{:S(2)}) collective-permute-start(f32[32,896]{1,0:T(8,128)S(1)} %shard_map.59.refs_6_.refs_2_), channel_id=1, source_target_pairs={{0,1},{1,0},{2,3},{3,2},{4,5},{5,4},{6,7},{7,6},{8,9},{9,8},{10,11... | collective-permute-start | bytes 344072 | tf_op jit(solution)/shard_map/ppermute | solution.py:35
  64.0 5.8 %collective-permute-start.27 = (f32[32,896]{1,0:T(8,128)S(1)}, f32[32,896]{1,0:T(8,128)S(1)}, u32[]{:S(2)}, u32[]{:S(2)}) collective-permute-start(f32[32,896]{1,0:T(8,128)S(1)} %shard_map.59.refs_6_.refs_2_), channel_id=1, source_target_pairs={{0,1},{1,0},{2,3},{3,2},{4,5},{5,4},{6,7},{7,6},{8,9},{9,8},{10,11... | collective-permute-start | bytes 344072 | tf_op jit(solution)/shard_map/ppermute | solution.py:35
  64.9 5.0 %collective-permute-start.29 = (f32[32,896]{1,0:T(8,128)S(1)}, f32[32,896]{1,0:T(8,128)S(1)}, u32[]{:S(2)}, u32[]{:S(2)}) collective-permute-start(f32[32,896]{1,0:T(8,128)S(1)} %shard_map.60.refs_7_.refs_2_), channel_id=1, source_target_pairs={{0,1},{1,0},{2,3},{3,2},{4,5},{5,4},{6,7},{7,6},{8,9},{9,8},{10,11... | collective-permute-start | bytes 344072 | tf_op jit(solution)/shard_map/ppermute | solution.py:35
  68.5 5.5 %collective-permute-start.30 = (f32[32,896]{1,0:T(8,128)S(1)}, f32[32,896]{1,0:T(8,128)S(1)}, u32[]{:S(2)}, u32[]{:S(2)}) collective-permute-start(f32[32,896]{1,0:T(8,128)S(1)} %shard_map.60.refs_7_.refs_2_), channel_id=1, source_target_pairs={{0,1},{1,0},{2,3},{3,2},{4,5},{5,4},{6,7},{7,6},{8,9},{9,8},{10,11... | collective-permute-start | bytes 344072 | tf_op jit(solution)/shard_map/ppermute | solution.py:35
  74.2 2.0 %collective-permute-start.31 = (f32[64,448]{1,0:T(8,128)S(1)}, f32[64,448]{1,0:T(8,128)S(1)}, u32[]{:S(2)}, u32[]{:S(2)}) collective-permute-start(f32[64,448]{1,0:T(8,128)S(1)} %shard_map.63), channel_id=1, source_target_pairs={{0,1},{1,0},{2,3},{3,2},{4,5},{5,4},{6,7},{7,6},{8,9},{9,8},{10,11... | collective-permute-start | bytes 344072 | tf_op jit(solution)/shard_map/ppermute | solution.py:46

commit v3 on v2

--- a/solution.py
+++ b/solution.py
@@ -202,6 +202,8 @@
     )
     got_offset = ship(offset, evens)
 
+    gives = []
+
     def step(c, xs, plan, got=(), after=(), alias=True):
         double = len(got) > 0
         count = len(xs)
@@ -210,15 +212,20 @@
             x_refs, refs = refs[:count], refs[count:]
             before_ref, matrix_ref, offset_ref = refs[:3]
             got_ref, got_offset_ref = refs[3:5] if double else (None, None)
-            step_kernel(c, plan, alias, x_refs, matrix_ref, offset_ref, got_ref, got_offset_ref, before_ref, refs[-1])
-
+            step_kernel(c, plan, alias, x_refs, matrix_ref, offset_ref, got_ref, got_offset_ref, before_ref, refs[-1 - len(gave)])
+            if gave:
+                y_ref, first = refs[-2], first_core()
+                refs[-1][...] = jnp.where(first, y_ref[:, part:], y_ref[:, :part])
+
+        gave = [] if alias else [shape((chunk, part), F32)]
         after = (ys[c - 1], *after)
-        (ys[c],) = call(
+        ys[c], *sent = call(
             kernel,
             (*xs, ys[c], matrix, offset, *got, *after),
-            [VMEM] * (count + 3 + len(got)) + [ANY] * len(after), [piece],
+            [VMEM] * (count + 3 + len(got)) + [ANY] * len(after), [piece, *gave],
             aliases={count: 0} if alias else None, flops=product * (1 + double),
         )
+        gives.extend(sent)
 
     def move(c, *cycles):
         return hop(ys[c], *cycles)
@@ -246,22 +253,17 @@
             xs = [move(c, *cycles)] + ([move(c, (odd - 2, odd - 1, odd - 7))] if last else [])
             step(c, xs, plan, got=(moved, got_offset), alias=not last)
 
-    def give_kernel(*refs):
-        y = jnp.concatenate([ref[...] for ref in refs[:CHUNKS]], axis=0)
-        refs[-1][...] = jnp.where(first_core(), y[:, part:], y[:, :part])
-
     def end_kernel(*refs):
         y = jnp.concatenate([ref[...] for ref in refs[:CHUNKS]], axis=0)
         first = first_core()
         mine = jnp.where(first, y[:, :part], y[:, part:])
-        taken = refs[CHUNKS][...]
+        taken = jnp.concatenate([ref[...] for ref in refs[CHUNKS:-1]], axis=0)
         rows = jnp.concatenate(
             [jnp.where(first, mine, taken), jnp.where(first, taken, mine)], axis=0
         )
         refs[-1][...] = rows.T
 
-    (give,) = call(give_kernel, tuple(ys), [VMEM] * CHUNKS, [shape((half, part), F32)])
-    (out,) = call(end_kernel, (*ys, swap_cores(give)), [VMEM] * (CHUNKS + 1), [shape((part, columns), F32)])
+    (out,) = call(end_kernel, (*ys, *map(swap_cores, gives)), [VMEM] * (2 * CHUNKS), [shape((part, columns), F32)])
     return out[None]
 
 

time: 77.2 us -> 77.5 us (level)
    ppermute x6 -> x7, waiting for transfers between devices: 3.01 us -> 3.2 us  [swap_cores(): return lax.ppermute(block, ('tm', 'row'), route)]
    pallas_call x28 -> x27, Pallas kernels: 2.55 us -> 2.68 us  [call(): pl.pallas_call(kernel, out_shape=tuple(outs), in_specs=specs, out_specs=t...]
    ppermute x6 -> x7, starting transfers between devices: 3.5 us -> 3.57 us  [swap_cores(): return lax.ppermute(block, ('tm', 'row'), route)]
  transfers between devices with their start and end apart: 32 -> 33, of which waited for: 16 -> 17; matrix products, arithmetic and copies ran while one was open for 0% -> 0% of each run, Pallas kernels for 2% -> 2%
where the time goes in v3:
time: 77.5 us; the launch traced here: 77.3 us
  waiting for transfers between devices  41.9 us (54%)
  starting transfers between devices  31.3 us (40%)
  Pallas kernels  2.68 us (3%)
  other arithmetic  1.34 us (2%)
    ppermute x2, waiting for transfers between devices, ship(): lax.ppermute(block, ('tm', 'row'), route_of({e: e + 1 for e in evens}, Fa...  25.3 us
    ppermute x24, starting transfers between devices, hop(): return lax.ppermute(block, ('tm', 'row'), route_of(to, True))  20.4 us
    ppermute x24, waiting for transfers between devices, hop(): return lax.ppermute(block, ('tm', 'row'), route_of(to, True))  13.3 us
    ppermute x2, starting transfers between devices, ship(): lax.ppermute(block, ('tm', 'row'), route_of({e: e + 1 for e in evens}, Fa...  7.31 us
    ppermute x7, starting transfers between devices, swap_cores(): return lax.ppermute(block, ('tm', 'row'), route)  3.57 us
    ppermute x7, waiting for transfers between devices, swap_cores(): return lax.ppermute(block, ('tm', 'row'), route)  3.2 us
    pallas_call x27, Pallas kernels, call(): pl.pallas_call(kernel, out_shape=tuple(outs), in_specs=specs, out_specs=t...  2.68 us
  transfers between devices with their start and end apart: 33, of which 17 were waited for; matrix products, arithmetic and copies ran while one was open for 0% of the time, Pallas kernels for 2%

profile of v3, /device:TPU:17, one launch (start us, length us, event | category | flops | bytes accessed | tf_op | source)
XLA Modules:
  0.0 77.3 jit_solution(12137107735655334554)
XLA Ops:
  0.0 1.3 %bitcast_convert_fusion = f32[448,896]{1,0:T(8,128)S(1)} fusion(bf16[1,448,896]{2,1,0:T(8,128)(2,1)} %param.3), kind=kLoop, calls=%fused_computation | loop fusion | flops 401408 | bytes 2408448 | tf_op jit(solution)/shard_map/convert_element_type | solution.py:189
  1.4 0.7 collective-permute-start.3
  2.1 3.2 %collective-permute-start.18 = (f32[448,896]{1,0:T(8,128)S(1)}, f32[448,896]{1,0:T(8,128)S(1)}, u32[]{:S(2)}, u32[]{:S(2)}) collective-permute-start(f32[448,896]{1,0:T(8,128)S(1)} %bitcast_convert_fusion), channel_id=1, source_target_pairs={{16,18},{17,19},{20,22},{21,23},{24,26},{25,27},{28,30},{29,31}} | collective-permute-start | bytes 4816904 | tf_op jit(solution)/shard_map/ppermute | solution.py:39
  5.3 0.4 collective-permute-start
  5.7 1.2 %collective-permute-done.other_start_ref = f32[448,128]{1,0:T(8,128)S(1)} collective-permute-done((f32[448,128]{1,0:T(8,128)S(1)}, f32[448,128]{1,0:T(8,128)S(1)}, u32[]{:S(2)}, u32[]{:S(2)}) %collective-permute-start) | collective-permute-done | bytes 229408 | tf_op jit(solution)/shard_map/ppermute | solution.py:46
  6.9 0.3 collective-permute-start.1
  7.2 0.2 collective-permute-start.4
  7.4 0.8 %collective-permute-done.1.got_ref = f32[64,448]{1,0:T(8,128)S(1)} collective-permute-done((f32[64,448]{1,0:T(8,128)S(1)}, f32[64,448]{1,0:T(8,128)S(1)}, u32[]{:S(2)}, u32[]{:S(2)}) %collective-permute-start.1) | collective-permute-done | bytes 114720 | tf_op jit(solution)/shard_map/ppermute | solution.py:46
  8.2 0.3 collective-permute-start.2
  8.5 0.2 collective-permute-start.6
  8.8 0.7 shard_map.39
  9.6 0.3 collective-permute-start.5
  9.9 0.2 collective-permute-start.8
  10.1 0.8 %collective-permute-done.5.refs_0_ = f32[32,896]{1,0:T(8,128)S(1)} collective-permute-done((f32[32,896]{1,0:T(8,128)S(1)}, f32[32,896]{1,0:T(8,128)S(1)}, u32[]{:S(2)}, u32[]{:S(2)}) %collective-permute-start.5) | collective-permute-done | bytes 114720 | tf_op jit(solution)/shard_map/ppermute | solution.py:35
  10.9 0.3 collective-permute-start.7
  11.2 0.2 collective-permute-start.10
  11.4 0.8 %collective-permute-done.7.refs_0_ = f32[32,896]{1,0:T(8,128)S(1)} collective-permute-done((f32[32,896]{1,0:T(8,128)S(1)}, f32[32,896]{1,0:T(8,128)S(1)}, u32[]{:S(2)}, u32[]{:S(2)}) %collective-permute-start.7) | collective-permute-done | bytes 114720 | tf_op jit(solution)/shard_map/ppermute | solution.py:35
  12.2 0.3 collective-permute-start.9
  12.7 0.8 %collective-permute-done.9.refs_0_ = f32[32,896]{1,0:T(8,128)S(1)} collective-permute-done((f32[32,896]{1,0:T(8,128)S(1)}, f32[32,896]{1,0:T(8,128)S(1)}, u32[]{:S(2)}, u32[]{:S(2)}) %collective-permute-start.9) | collective-permute-done | bytes 114720 | tf_op jit(solution)/shard_map/ppermute | solution.py:35
  13.5 0.3 collective-permute-start.11
  13.8 0.2 collective-permute-start.14
  14.1 0.8 %collective-permute-done.11.refs_0_ = f32[32,896]{1,0:T(8,128)S(1)} collective-permute-done((f32[32,896]{1,0:T(8,128)S(1)}, f32[32,896]{1,0:T(8,128)S(1)}, u32[]{:S(2)}, u32[]{:S(2)}) %collective-permute-start.11) | collective-permute-done | bytes 114720 | tf_op jit(solution)/shard_map/ppermute | solution.py:35
  14.9 0.3 collective-permute-start.13
  15.4 0.8 %collective-permute-done.13.refs_0_ = f32[32,896]{1,0:T(8,128)S(1)} collective-permute-done((f32[32,896]{1,0:T(8,128)S(1)}, f32[32,896]{1,0:T(8,128)S(1)}, u32[]{:S(2)}, u32[]{:S(2)}) %collective-permute-start.13) | collective-permute-done | bytes 114720 | tf_op jit(solution)/shard_map/ppermute | solution.py:35
  16.2 0.3 collective-permute-start.15
  16.5 1.0 %collective-permute-done.15.refs_0_ = f32[32,896]{1,0:T(8,128)S(1)} collective-permute-done((f32[32,896]{1,0:T(8,128)S(1)}, f32[32,896]{1,0:T(8,128)S(1)}, u32[]{:S(2)}, u32[]{:S(2)}) %collective-permute-start.15) | collective-permute-done | bytes 114720 | tf_op jit(solution)/shard_map/ppermute | solution.py:35
  17.5 22.1 %collective-permute-done.18.refs_0_ = f32[448,896]{1,0:T(8,128)S(1)} collective-permute-done((f32[448,896]{1,0:T(8,128)S(1)}, f32[448,896]{1,0:T(8,128)S(1)}, u32[]{:S(2)}, u32[]{:S(2)}) %collective-permute-start.18) | collective-permute-done | bytes 1605664 | tf_op jit(solution)/shard_map/ppermute | solution.py:39
  39.6 0.9 %collective-permute-start.19 = (f32[448,896]{1,0:T(8,128)S(1)}, f32[448,896]{1,0:T(8,128)S(1)}, u32[]{:S(2)}, u32[]{:S(2)}) collective-permute-start(f32[448,896]{1,0:T(8,128)S(1)} %gate.1.own_ref), channel_id=1, source_target_pairs={{0,1},{1,0},{2,3},{3,2},{4,5},{5,4},{6,7},{7,6},{8,9},{9,8},{10,11... | collective-permute-start | bytes 4816904 | tf_op jit(solution)/shard_map/ppermute | solution.py:46
  40.5 4.1 %collective-permute-start.20 = (f32[64,896]{1,0:T(8,128)S(1)}, f32[64,896]{1,0:T(8,128)S(1)}, u32[]{:S(2)}, u32[]{:S(2)}) collective-permute-start(f32[64,896]{1,0:T(8,128)S(1)} %get-tuple-element.19.refs_3_.refs_4_), channel_id=1, source_target_pairs={{16,18},{17,19},{20,22},{21,23},{24,26},{25,27},{28,30},{29,31}} | collective-permute-start | bytes 688136 | tf_op jit(solution)/shard_map/ppermute | solution.py:39
  44.6 0.3 collective-permute-start.21
  45.0 0.2 collective-permute-start.17
  45.2 0.8 %collective-permute-done.21.refs_0_ = f32[32,896]{1,0:T(8,128)S(1)} collective-permute-done((f32[32,896]{1,0:T(8,128)S(1)}, f32[32,896]{1,0:T(8,128)S(1)}, u32[]{:S(2)}, u32[]{:S(2)}) %collective-permute-start.21) | collective-permute-done | bytes 114720 | tf_op jit(solution)/shard_map/ppermute | solution.py:35
  46.0 0.3 collective-permute-start.23
  46.3 3.2 %collective-permute-done.20.refs_5_.refs_6_ = f32[64,896]{1,0:T(8,128)S(1)} collective-permute-done((f32[64,896]{1,0:T(8,128)S(1)}, f32[64,896]{1,0:T(8,128)S(1)}, u32[]{:S(2)}, u32[]{:S(2)}) %collective-permute-start.20) | collective-permute-done | bytes 229408 | tf_op jit(solution)/shard_map/ppermute | solution.py:39
  49.6 6.8 %collective-permute-start.25 = (f32[32,896]{1,0:T(8,128)S(1)}, f32[32,896]{1,0:T(8,128)S(1)}, u32[]{:S(2)}, u32[]{:S(2)}) collective-permute-start(f32[32,896]{1,0:T(8,128)S(1)} %shard_map.56.refs_6_.refs_1_), channel_id=1, source_target_pairs={{0,14},{1,15},{2,3},{3,2},{4,5},{5,4},{6,7},{7,6},{8,9},{9,8},{10,... | collective-permute-start | bytes 344072 | tf_op jit(solution)/shard_map/ppermute | solution.py:35
  56.4 2.5 %collective-permute-done.22.refs_0_ = f32[32,896]{1,0:T(8,128)S(1)} collective-permute-done((f32[32,896]{1,0:T(8,128)S(1)}, f32[32,896]{1,0:T(8,128)S(1)}, u32[]{:S(2)}, u32[]{:S(2)}) %collective-permute-start.22) | collective-permute-done | bytes 114720 | tf_op jit(solution)/shard_map/ppermute | solution.py:35
  58.9 0.4 shard_map.57.refs_6_.refs_1_
  59.2 1.8 %collective-permute-start.24 = (f32[32,896]{1,0:T(8,128)S(1)}, f32[32,896]{1,0:T(8,128)S(1)}, u32[]{:S(2)}, u32[]{:S(2)}) collective-permute-start(f32[32,896]{1,0:T(8,128)S(1)} %shard_map.57.refs_6_.refs_1_), channel_id=1, source_target_pairs={{0,1},{1,0},{2,3},{3,2},{4,18},{5,19},{6,7},{7,6},{8,9},{9,8},{10,... | collective-permute-start | bytes 344072 | tf_op jit(solution)/shard_map/ppermute | solution.py:35
  61.0 0.4 shard_map.58.refs_6_.refs_1_
  61.4 2.5 %collective-permute-start.28 = (f32[32,896]{1,0:T(8,128)S(1)}, f32[32,896]{1,0:T(8,128)S(1)}, u32[]{:S(2)}, u32[]{:S(2)}) collective-permute-start(f32[32,896]{1,0:T(8,128)S(1)} %shard_map.58.refs_6_.refs_1_), channel_id=1, source_target_pairs={{0,1},{1,0},{2,3},{3,2},{4,18},{5,19},{6,7},{7,6},{8,9},{9,8},{10,... | collective-permute-start | bytes 344072 | tf_op jit(solution)/shard_map/ppermute | solution.py:35
  64.0 0.8 %collective-permute-done.28.refs_0_ = f32[32,896]{1,0:T(8,128)S(1)} collective-permute-done((f32[32,896]{1,0:T(8,128)S(1)}, f32[32,896]{1,0:T(8,128)S(1)}, u32[]{:S(2)}, u32[]{:S(2)}) %collective-permute-start.28) | collective-permute-done | bytes 114720 | tf_op jit(solution)/shard_map/ppermute | solution.py:35
  64.9 3.6 %collective-permute-start.29 = (f32[32,896]{1,0:T(8,128)S(1)}, f32[32,896]{1,0:T(8,128)S(1)}, u32[]{:S(2)}, u32[]{:S(2)}) collective-permute-start(f32[32,896]{1,0:T(8,128)S(1)} %shard_map.60.refs_7_.refs_2_), channel_id=1, source_target_pairs={{0,1},{1,0},{2,3},{3,2},{4,5},{5,4},{6,7},{7,6},{8,9},{9,8},{10,11... | collective-permute-start | bytes 344072 | tf_op jit(solution)/shard_map/ppermute | solution.py:35
  68.5 1.4 %collective-permute-start.30 = (f32[32,896]{1,0:T(8,128)S(1)}, f32[32,896]{1,0:T(8,128)S(1)}, u32[]{:S(2)}, u32[]{:S(2)}) collective-permute-start(f32[32,896]{1,0:T(8,128)S(1)} %shard_map.60.refs_7_.refs_2_), channel_id=1, source_target_pairs={{0,1},{1,0},{2,3},{3,2},{4,5},{5,4},{6,7},{7,6},{8,9},{9,8},{10,11... | collective-permute-start | bytes 344072 | tf_op jit(solution)/shard_map/ppermute | solution.py:35
  70.1 4.0 %collective-permute-done.30.refs_1_ = f32[32,896]{1,0:T(8,128)S(1)} collective-permute-done((f32[32,896]{1,0:T(8,128)S(1)}, f32[32,896]{1,0:T(8,128)S(1)}, u32[]{:S(2)}, u32[]{:S(2)}) %collective-permute-start.30) | collective-permute-done | bytes 114720 | tf_op jit(solution)/shard_map/ppermute | solution.py:35
  74.2 1.0 %collective-permute-start.32 = (f32[32,448]{1,0:T(8,128)S(1)}, f32[32,448]{1,0:T(8,128)S(1)}, u32[]{:S(2)}, u32[]{:S(2)}) collective-permute-start(f32[32,448]{1,0:T(8,128)S(1)} %get-tuple-element.24), channel_id=1, source_target_pairs={{0,1},{1,0},{2,3},{3,2},{4,5},{5,4},{6,7},{7,6},{8,9},{9,8},{10,11... | collective-permute-start | bytes 172040 | tf_op jit(solution)/shard_map/ppermute | solution.py:46
  75.3 0.8 %collective-permute-done.32.refs_3_ = f32[32,448]{1,0:T(8,128)S(1)} collective-permute-done((f32[32,448]{1,0:T(8,128)S(1)}, f32[32,448]{1,0:T(8,128)S(1)}, u32[]{:S(2)}, u32[]{:S(2)}) %collective-permute-start.32) | collective-permute-done | bytes 57376 | tf_op jit(solution)/shard_map/ppermute | solution.py:46
  76.1 0.4 collective-permute-done.31.refs_2_
  76.4 0.9 %shard_map.63 = f32[448,128]{1,0:T(8,128)} custom-call(f32[32,896]{1,0:T(8,128)S(1)} %get-tuple-element.21.refs_7_.refs_0_, f32[32,896]{1,0:T(8,128)S(1)} %get-tuple-element.22.refs_1_, f32[32,448]{1,0:T(8,128)S(1)} %collective-permute-done.31.refs_2_, f32[32,448]{1,0:T(8,128)S(1)} %collective-permute-done.32.refs_3_), custom_call_target="tpu_custom_call" | custom-call | bytes 229376 | tf_op jit(solution)/shard_map/pallas_call | solution.py:51
  (53 shorter events, 1.1 us)
Async XLA Ops:
  0.0 6.9 %copy-start = (bf16[1,448,896]{2,1,0:T(8,128)(2,1)S(1)}, bf16[1,448,896]{2,1,0:T(8,128)(2,1)}, u32[]{:S(2)}) copy-start(bf16[1,448,896]{2,1,0:T(8,128)(2,1)} %param.3) | copy-start | bytes 2408452
  0.0 5.3 %copy-start.2 = (f32[448,128]{1,0:T(8,128)S(1)}, f32[448,128]{1,0:T(8,128)}, u32[]{:S(2)}) copy-start(f32[448,128]{1,0:T(8,128)} %start_ref.1) | copy-start | bytes 688132
  0.0 6.9 %copy-start.1 = (f32[1,448,128]{2,1,0:T(8,128)S(1)}, f32[1,448,128]{2,1,0:T(8,128)}, u32[]{:S(2)}) copy-start(f32[1,448,128]{2,1,0:T(8,128)} %param.4) | copy-start | bytes 688132
  1.4 7.4 %collective-permute-start.3 = (f32[448,896]{1,0:T(8,128)S(1)}, f32[448,896]{1,0:T(8,128)S(1)}, u32[]{:S(2)}, u32[]{:S(2)}) collective-permute-start(f32[448,896]{1,0:T(8,128)S(1)} %bitcast_convert_fusion), channel_id=1, source_target_pairs={{0,1},{1,0},{2,3},{3,2},{4,5},{5,4},{6,7},{7,6},{8,9},{9,8},{10,11... | collective-permute-start | bytes 4816904 | tf_op jit(solution)/shard_map/ppermute | solution.py:46
  2.1 37.5 %collective-permute-start.18 = (f32[448,896]{1,0:T(8,128)S(1)}, f32[448,896]{1,0:T(8,128)S(1)}, u32[]{:S(2)}, u32[]{:S(2)}) collective-permute-start(f32[448,896]{1,0:T(8,128)S(1)} %bitcast_convert_fusion), channel_id=1, source_target_pairs={{16,18},{17,19},{20,22},{21,23},{24,26},{25,27},{28,30},{29,31}} | collective-permute-start | bytes 4816904 | tf_op jit(solution)/shard_map/ppermute | solution.py:39
  5.3 1.6 %collective-permute-start = (f32[448,128]{1,0:T(8,128)S(1)}, f32[448,128]{1,0:T(8,128)S(1)}, u32[]{:S(2)}, u32[]{:S(2)}) collective-permute-start(f32[448,128]{1,0:T(8,128)S(1)} %copy-done.2), channel_id=1, source_target_pairs={{0,1},{1,0},{2,3},{3,2},{4,5},{5,4},{6,7},{7,6},{8,9},{9,8},{10,11... | collective-permute-start | bytes 688136 | tf_op jit(solution)/shard_map/ppermute | solution.py:46
  6.9 1.3 %collective-permute-start.1 = (f32[64,448]{1,0:T(8,128)S(1)}, f32[64,448]{1,0:T(8,128)S(1)}, u32[]{:S(2)}, u32[]{:S(2)}) collective-permute-start(f32[64,448]{1,0:T(8,128)S(1)} %get-tuple-element.16), channel_id=1, source_target_pairs={{0,1},{1,0},{2,3},{3,2},{4,5},{5,4},{6,7},{7,6},{8,9},{9,8},{10,11... | collective-permute-start | bytes 344072 | tf_op jit(solution)/shard_map/ppermute | solution.py:46
  7.2 1.6 %collective-permute-start.4 = (f32[448,128]{1,0:T(8,128)S(1)}, f32[448,128]{1,0:T(8,128)S(1)}, u32[]{:S(2)}, u32[]{:S(2)}) collective-permute-start(f32[448,128]{1,0:T(8,128)S(1)} %bitcast.7), channel_id=1, source_target_pairs={{0,1},{1,0},{2,3},{3,2},{4,5},{5,4},{6,7},{7,6},{8,9},{9,8},{10,11... | collective-permute-start | bytes 688136 | tf_op jit(solution)/shard_map/ppermute | solution.py:46
  8.2 1.3 %collective-permute-start.2 = (f32[32,896]{1,0:T(8,128)S(1)}, f32[32,896]{1,0:T(8,128)S(1)}, u32[]{:S(2)}, u32[]{:S(2)}) collective-permute-start(f32[32,896]{1,0:T(8,128)S(1)} %get-tuple-element.17.refs_1_), channel_id=1, source_target_pairs={{0,2},{1,3},{2,0},{3,1},{4,5},{5,4},{6,7},{7,6},{8,9},{9,8},{10,11... | collective-permute-start | bytes 344072 | tf_op jit(solution)/shard_map/ppermute | solution.py:35
  8.5 1.3 %collective-permute-start.6 = (f32[32,896]{1,0:T(8,128)S(1)}, f32[32,896]{1,0:T(8,128)S(1)}, u32[]{:S(2)}, u32[]{:S(2)}) collective-permute-start(f32[32,896]{1,0:T(8,128)S(1)} %get-tuple-element.20.refs_4_.refs_1_), channel_id=1, source_target_pairs={{0,2},{1,3},{2,0},{3,1},{4,5},{5,4},{6,7},{7,6},{8,9},{9,8},{10,11... | collective-permute-start | bytes 344072 | tf_op jit(solution)/shard_map/ppermute | solution.py:35
  9.6 1.3 %collective-permute-start.5 = (f32[32,896]{1,0:T(8,128)S(1)}, f32[32,896]{1,0:T(8,128)S(1)}, u32[]{:S(2)}, u32[]{:S(2)}) collective-permute-start(f32[32,896]{1,0:T(8,128)S(1)} %shard_map.40.refs_4_.refs_1_), channel_id=1, source_target_pairs={{0,1},{1,0},{2,4},{3,5},{4,2},{5,3},{6,7},{7,6},{8,9},{9,8},{10,11... | collective-permute-start | bytes 344072 | tf_op jit(solution)/shard_map/ppermute | solution.py:35
  9.9 1.3 %collective-permute-start.8 = (f32[32,896]{1,0:T(8,128)S(1)}, f32[32,896]{1,0:T(8,128)S(1)}, u32[]{:S(2)}, u32[]{:S(2)}) collective-permute-start(f32[32,896]{1,0:T(8,128)S(1)} %shard_map.41.refs_4_.refs_1_), channel_id=1, source_target_pairs={{0,1},{1,0},{2,4},{3,5},{4,2},{5,3},{6,7},{7,6},{8,9},{9,8},{10,11... | collective-permute-start | bytes 344072 | tf_op jit(solution)/shard_map/ppermute | solution.py:35
  10.9 1.3 %collective-permute-start.7 = (f32[32,896]{1,0:T(8,128)S(1)}, f32[32,896]{1,0:T(8,128)S(1)}, u32[]{:S(2)}, u32[]{:S(2)}) collective-permute-start(f32[32,896]{1,0:T(8,128)S(1)} %shard_map.42.refs_4_.refs_1_), channel_id=1, source_target_pairs={{0,1},{1,0},{2,3},{3,2},{4,6},{5,7},{6,4},{7,5},{8,9},{9,8},{10,11... | collective-permute-start | bytes 344072 | tf_op jit(solution)/shard_map/ppermute | solution.py:35
  11.2 1.3 %collective-permute-start.10 = (f32[32,896]{1,0:T(8,128)S(1)}, f32[32,896]{1,0:T(8,128)S(1)}, u32[]{:S(2)}, u32[]{:S(2)}) collective-permute-start(f32[32,896]{1,0:T(8,128)S(1)} %shard_map.43.refs_4_.refs_1_), channel_id=1, source_target_pairs={{0,1},{1,0},{2,3},{3,2},{4,6},{5,7},{6,4},{7,5},{8,9},{9,8},{10,11... | collective-permute-start | bytes 344072 | tf_op jit(solution)/shard_map/ppermute | solution.py:35
  12.2 1.3 %collective-permute-start.9 = (f32[32,896]{1,0:T(8,128)S(1)}, f32[32,896]{1,0:T(8,128)S(1)}, u32[]{:S(2)}, u32[]{:S(2)}) collective-permute-start(f32[32,896]{1,0:T(8,128)S(1)} %shard_map.44.refs_4_.refs_1_), channel_id=1, source_target_pairs={{0,1},{1,0},{2,3},{3,2},{4,5},{5,4},{6,8},{7,9},{8,6},{9,7},{10,11... | collective-permute-start | bytes 344072 | tf_op jit(solution)/shard_map/ppermute | solution.py:35
  12.5 1.3 %collective-permute-start.12 = (f32[32,896]{1,0:T(8,128)S(1)}, f32[32,896]{1,0:T(8,128)S(1)}, u32[]{:S(2)}, u32[]{:S(2)}) collective-permute-start(f32[32,896]{1,0:T(8,128)S(1)} %shard_map.45.refs_4_.refs_1_), channel_id=1, source_target_pairs={{0,1},{1,0},{2,3},{3,2},{4,5},{5,4},{6,8},{7,9},{8,6},{9,7},{10,11... | collective-permute-start | bytes 344072 | tf_op jit(solution)/shard_map/ppermute | solution.py:35
  13.5 1.3 %collective-permute-start.11 = (f32[32,896]{1,0:T(8,128)S(1)}, f32[32,896]{1,0:T(8,128)S(1)}, u32[]{:S(2)}, u32[]{:S(2)}) collective-permute-start(f32[32,896]{1,0:T(8,128)S(1)} %shard_map.46.refs_4_.refs_1_), channel_id=1, source_target_pairs={{0,1},{1,0},{2,3},{3,2},{4,5},{5,4},{6,7},{7,6},{8,10},{9,11},{10,... | collective-permute-start | bytes 344072 | tf_op jit(solution)/shard_map/ppermute | solution.py:35
  13.8 1.3 %collective-permute-start.14 = (f32[32,896]{1,0:T(8,128)S(1)}, f32[32,896]{1,0:T(8,128)S(1)}, u32[]{:S(2)}, u32[]{:S(2)}) collective-permute-start(f32[32,896]{1,0:T(8,128)S(1)} %shard_map.47.refs_4_.refs_1_), channel_id=1, source_target_pairs={{0,1},{1,0},{2,3},{3,2},{4,5},{5,4},{6,7},{7,6},{8,10},{9,11},{10,... | collective-permute-start | bytes 344072 | tf_op jit(solution)/shard_map/ppermute | solution.py:35
  14.9 1.3 %collective-permute-start.13 = (f32[32,896]{1,0:T(8,128)S(1)}, f32[32,896]{1,0:T(8,128)S(1)}, u32[]{:S(2)}, u32[]{:S(2)}) collective-permute-start(f32[32,896]{1,0:T(8,128)S(1)} %shard_map.48.refs_4_.refs_1_), channel_id=1, source_target_pairs={{0,1},{1,0},{2,3},{3,2},{4,5},{5,4},{6,7},{7,6},{8,9},{9,8},{10,12... | collective-permute-start | bytes 344072 | tf_op jit(solution)/shard_map/ppermute | solution.py:35
  15.2 1.3 %collective-permute-start.16 = (f32[32,896]{1,0:T(8,128)S(1)}, f32[32,896]{1,0:T(8,128)S(1)}, u32[]{:S(2)}, u32[]{:S(2)}) collective-permute-start(f32[32,896]{1,0:T(8,128)S(1)} %shard_map.49.refs_4_.refs_1_), channel_id=1, source_target_pairs={{0,1},{1,0},{2,3},{3,2},{4,5},{5,4},{6,7},{7,6},{8,9},{9,8},{10,12... | collective-permute-start | bytes 344072 | tf_op jit(solution)/shard_map/ppermute | solution.py:35
  16.2 1.3 %collective-permute-start.15 = (f32[32,896]{1,0:T(8,128)S(1)}, f32[32,896]{1,0:T(8,128)S(1)}, u32[]{:S(2)}, u32[]{:S(2)}) collective-permute-start(f32[32,896]{1,0:T(8,128)S(1)} %shard_map.50.refs_4_.refs_1_), channel_id=1, source_target_pairs={{0,1},{1,0},{2,3},{3,2},{4,5},{5,4},{6,7},{7,6},{8,9},{9,8},{10,11... | collective-permute-start | bytes 344072 | tf_op jit(solution)/shard_map/ppermute | solution.py:35
  39.6 6.7 %collective-permute-start.19 = (f32[448,896]{1,0:T(8,128)S(1)}, f32[448,896]{1,0:T(8,128)S(1)}, u32[]{:S(2)}, u32[]{:S(2)}) collective-permute-start(f32[448,896]{1,0:T(8,128)S(1)} %gate.1.own_ref), channel_id=1, source_target_pairs={{0,1},{1,0},{2,3},{3,2},{4,5},{5,4},{6,7},{7,6},{8,9},{9,8},{10,11... | collective-permute-start | bytes 4816904 | tf_op jit(solution)/shard_map/ppermute | solution.py:46
  40.5 9.0 %collective-permute-start.20 = (f32[64,896]{1,0:T(8,128)S(1)}, f32[64,896]{1,0:T(8,128)S(1)}, u32[]{:S(2)}, u32[]{:S(2)}) collective-permute-start(f32[64,896]{1,0:T(8,128)S(1)} %get-tuple-element.19.refs_3_.refs_4_), channel_id=1, source_target_pairs={{16,18},{17,19},{20,22},{21,23},{24,26},{25,27},{28,30},{29,31}} | collective-permute-start | bytes 688136 | tf_op jit(solution)/shard_map/ppermute | solution.py:39
  44.6 1.4 %collective-permute-start.21 = (f32[32,896]{1,0:T(8,128)S(1)}, f32[32,896]{1,0:T(8,128)S(1)}, u32[]{:S(2)}, u32[]{:S(2)}) collective-permute-start(f32[32,896]{1,0:T(8,128)S(1)} %shard_map.51.refs_4_.refs_1_), channel_id=1, source_target_pairs={{0,1},{1,0},{2,3},{3,2},{4,5},{5,4},{6,7},{7,6},{8,9},{9,8},{10,11... | collective-permute-start | bytes 344072 | tf_op jit(solution)/shard_map/ppermute | solution.py:35
  45.0 4.6 %collective-permute-start.17 = (f32[32,896]{1,0:T(8,128)S(1)}, f32[32,896]{1,0:T(8,128)S(1)}, u32[]{:S(2)}, u32[]{:S(2)}) collective-permute-start(f32[32,896]{1,0:T(8,128)S(1)} %shard_map.52.refs_1_.refs_4_), channel_id=1, source_target_pairs={{0,1},{1,0},{2,14},{3,15},{4,5},{5,4},{6,7},{7,6},{8,9},{9,8},{10,... | collective-permute-start | bytes 344072 | tf_op jit(solution)/shard_map/ppermute | solution.py:35
  46.0 3.5 %collective-permute-start.23 = (f32[32,896]{1,0:T(8,128)S(1)}, f32[32,896]{1,0:T(8,128)S(1)}, u32[]{:S(2)}, u32[]{:S(2)}) collective-permute-start(f32[32,896]{1,0:T(8,128)S(1)} %shard_map.54.refs_6_.refs_1_), channel_id=1, source_target_pairs={{0,1},{1,0},{2,14},{3,15},{4,5},{5,4},{6,7},{7,6},{8,9},{9,8},{10,... | collective-permute-start | bytes 344072 | tf_op jit(solution)/shard_map/ppermute | solution.py:35
  49.5 9.3 %collective-permute-start.22 = (f32[32,896]{1,0:T(8,128)S(1)}, f32[32,896]{1,0:T(8,128)S(1)}, u32[]{:S(2)}, u32[]{:S(2)}) collective-permute-start(f32[32,896]{1,0:T(8,128)S(1)} %shard_map.55.refs_6_.refs_1_), channel_id=1, source_target_pairs={{0,14},{1,15},{2,3},{3,2},{4,5},{5,4},{6,7},{7,6},{8,9},{9,8},{10,... | collective-permute-start | bytes 344072 | tf_op jit(solution)/shard_map/ppermute | solution.py:35
  49.6 11.5 %collective-permute-start.25 = (f32[32,896]{1,0:T(8,128)S(1)}, f32[32,896]{1,0:T(8,128)S(1)}, u32[]{:S(2)}, u32[]{:S(2)}) collective-permute-start(f32[32,896]{1,0:T(8,128)S(1)} %shard_map.56.refs_6_.refs_1_), channel_id=1, source_target_pairs={{0,14},{1,15},{2,3},{3,2},{4,5},{5,4},{6,7},{7,6},{8,9},{9,8},{10,... | collective-permute-start | bytes 344072 | tf_op jit(solution)/shard_map/ppermute | solution.py:35
  59.2 4.7 %collective-permute-start.24 = (f32[32,896]{1,0:T(8,128)S(1)}, f32[32,896]{1,0:T(8,128)S(1)}, u32[]{:S(2)}, u32[]{:S(2)}) collective-permute-start(f32[32,896]{1,0:T(8,128)S(1)} %shard_map.57.refs_6_.refs_1_), channel_id=1, source_target_pairs={{0,1},{1,0},{2,3},{3,2},{4,18},{5,19},{6,7},{7,6},{8,9},{9,8},{10,... | collective-permute-start | bytes 344072 | tf_op jit(solution)/shard_map/ppermute | solution.py:35
  61.4 3.5 %collective-permute-start.28 = (f32[32,896]{1,0:T(8,128)S(1)}, f32[32,896]{1,0:T(8,128)S(1)}, u32[]{:S(2)}, u32[]{:S(2)}) collective-permute-start(f32[32,896]{1,0:T(8,128)S(1)} %shard_map.58.refs_6_.refs_1_), channel_id=1, source_target_pairs={{0,1},{1,0},{2,3},{3,2},{4,18},{5,19},{6,7},{7,6},{8,9},{9,8},{10,... | collective-permute-start | bytes 344072 | tf_op jit(solution)/shard_map/ppermute | solution.py:35
  63.9 6.0 %collective-permute-start.26 = (f32[32,896]{1,0:T(8,128)S(1)}, f32[32,896]{1,0:T(8,128)S(1)}, u32[]{:S(2)}, u32[]{:S(2)}) collective-permute-start(f32[32,896]{1,0:T(8,128)S(1)} %shard_map.59.refs_6_.refs_2_), channel_id=1, source_target_pairs={{0,1},{1,0},{2,3},{3,2},{4,5},{5,4},{6,7},{7,6},{8,9},{9,8},{10,11... | collective-permute-start | bytes 344072 | tf_op jit(solution)/shard_map/ppermute | solution.py:35
  64.0 5.8 %collective-permute-start.27 = (f32[32,896]{1,0:T(8,128)S(1)}, f32[32,896]{1,0:T(8,128)S(1)}, u32[]{:S(2)}, u32[]{:S(2)}) collective-permute-start(f32[32,896]{1,0:T(8,128)S(1)} %shard_map.59.refs_6_.refs_2_), channel_id=1, source_target_pairs={{0,1},{1,0},{2,3},{3,2},{4,5},{5,4},{6,7},{7,6},{8,9},{9,8},{10,11... | collective-permute-start | bytes 344072 | tf_op jit(solution)/shard_map/ppermute | solution.py:35
  64.9 5.2 %collective-permute-start.29 = (f32[32,896]{1,0:T(8,128)S(1)}, f32[32,896]{1,0:T(8,128)S(1)}, u32[]{:S(2)}, u32[]{:S(2)}) collective-permute-start(f32[32,896]{1,0:T(8,128)S(1)} %shard_map.60.refs_7_.refs_2_), channel_id=1, source_target_pairs={{0,1},{1,0},{2,3},{3,2},{4,5},{5,4},{6,7},{7,6},{8,9},{9,8},{10,11... | collective-permute-start | bytes 344072 | tf_op jit(solution)/shard_map/ppermute | solution.py:35
  68.5 5.5 %collective-permute-start.30 = (f32[32,896]{1,0:T(8,128)S(1)}, f32[32,896]{1,0:T(8,128)S(1)}, u32[]{:S(2)}, u32[]{:S(2)}) collective-permute-start(f32[32,896]{1,0:T(8,128)S(1)} %shard_map.60.refs_7_.refs_2_), channel_id=1, source_target_pairs={{0,1},{1,0},{2,3},{3,2},{4,5},{5,4},{6,7},{7,6},{8,9},{9,8},{10,11... | collective-permute-start | bytes 344072 | tf_op jit(solution)/shard_map/ppermute | solution.py:35
  74.2 1.9 %collective-permute-start.32 = (f32[32,448]{1,0:T(8,128)S(1)}, f32[32,448]{1,0:T(8,128)S(1)}, u32[]{:S(2)}, u32[]{:S(2)}) collective-permute-start(f32[32,448]{1,0:T(8,128)S(1)} %get-tuple-element.24), channel_id=1, source_target_pairs={{0,1},{1,0},{2,3},{3,2},{4,5},{5,4},{6,7},{7,6},{8,9},{9,8},{10,11... | collective-permute-start | bytes 172040 | tf_op jit(solution)/shard_map/ppermute | solution.py:46
  75.2 1.3 %collective-permute-start.31 = (f32[32,448]{1,0:T(8,128)S(1)}, f32[32,448]{1,0:T(8,128)S(1)}, u32[]{:S(2)}, u32[]{:S(2)}) collective-permute-start(f32[32,448]{1,0:T(8,128)S(1)} %get-tuple-element.23), channel_id=1, source_target_pairs={{0,1},{1,0},{2,3},{3,2},{4,5},{5,4},{6,7},{7,6},{8,9},{9,8},{10,11... | collective-permute-start | bytes 172040 | tf_op jit(solution)/shard_map/ppermute | solution.py:46
